TPU v7x, 256 devices: a whole 4x4x8 slice. The times are simulated.
256 devices in a mesh: body: 2 (over x_hi), gx: 32 (over y, z), yz: 4 (over x_lo, core).
Axes of the slice: x: 4 (x_hi: 2, x_lo: 2; x = x_hi * 2 + x_lo), y: 4, z: 8, core: 2. Of those that a mesh axis runs over, the one named last changes fastest.
Arguments:
- displacement: float32 [2, 3, 512, 256, 128], P('body', None, 'gx', 'yz'), may hold values from -1.75 to 1.75
- velocity: float32 [2, 3, 512, 256, 128], P('body', None, 'gx', 'yz'), may hold values from -3 to 3
- material: int32 [2, 512, 256, 128], P('body', 'gx', 'yz'), may hold values from 0 to 7
- moduli: float32 [8], replicated, may hold values from 0.5 to 2
- density: float32 [8], replicated, may hold values from 1 to 4
- partner: int32 [256], replicated, may hold values from 0 to 255, as said below
- active: int32 [256], replicated, may hold values 0 or 1
Outputs:
- final_displacement: float32 [2, 3, 512, 256, 128], P('body', None, 'gx', 'yz')
- final_velocity: float32 [2, 3, 512, 256, 128], P('body', None, 'gx', 'yz')
Inputs may be any that keep to these rules, and one draw needn't show every extreme that they name: partner is a permutation of the rows of body 1's face; in every aligned block of 64 rows of partner, exactly 32 values lie in the same-numbered block of 64 rows and the others in the next block, the last block's next being the first.
All inputs are finite; a program needn't handle non-finite values.
Results may differ from a plain program's by a relative error of at most 0.0001.
Values sent between devices are 32-bit elements; how exact they have to be, the bound alone decides.
A program may use at most 64 MiB of HBM per device.

v0:
```python
import math

import jax
import jax.numpy as jnp
from jax import lax
from jax.sharding import PartitionSpec as P

STEPS = 4


STEP_TIME = 0.2
YIELD_SPAN = 0.5
PENALTY = 4.0
SOFT_WIDTH = 0.1
KERNEL_WIDTH = 1.5


def passed_along(block, axis, distance):
    devices = range(lax.axis_size(axis))
    route = [(i - distance, i) for i in devices if i - distance in devices]
    return lax.ppermute(block, axis, route)


def padded(block, sides, width):
    for axis, dim in sides:
        count = lax.axis_size(axis)
        forward = [(i, i + 1) for i in range(count - 1)]
        backward = [(target, source) for source, target in forward]
        low = lax.ppermute(
            lax.slice_in_dim(block, block.shape[dim] - width, None, axis=dim), axis, forward
        )
        high = lax.ppermute(lax.slice_in_dim(block, 0, width, axis=dim), axis, backward)
        block = jnp.concatenate([low, block, high], axis=dim)
    return block


def shifted_2(value, axis, steps):
    count = lax.axis_size(axis)
    pairs = [(source, (source + steps) % count) for source in range(count)]
    return lax.ppermute(value, axis, pairs)


def tension(stretch):
    return YIELD_SPAN * jnp.tanh(stretch / YIELD_SPAN)


def pair_pressure(own_surface, far_surface):
    column = jnp.arange(own_surface.shape[-1]).astype(jnp.float32)
    opening = -own_surface[0][:, :, None] - far_surface[0][:, None, :]
    along_z = (column + own_surface[2])[:, :, None] - (column + far_surface[2])[:, None, :]
    along_y = own_surface[1][:, :, None] - far_surface[1][:, None, :]
    weight = jnp.exp(-(along_y * along_y + along_z * along_z) / (2.0 * KERNEL_WIDTH * KERNEL_WIDTH))
    return weight * (PENALTY * SOFT_WIDTH) * jax.nn.softplus(-opening / SOFT_WIDTH)


def axis_forces(displace, stiffness, dimension):
    extent = displace.shape[dimension]
    zero_plane = jnp.zeros_like(lax.slice_in_dim(displace, 0, 1, axis=dimension))
    ahead = jnp.concatenate(
        [lax.slice_in_dim(displace, 1, extent, axis=dimension), zero_plane], axis=dimension
    )
    pulls = stiffness * tension(ahead - displace)
    behind = jnp.concatenate(
        [zero_plane, lax.slice_in_dim(pulls, 0, extent - 1, axis=dimension)], axis=dimension
    )
    return pulls - behind


def lookup(material, values_table):
    result = jnp.zeros(material.shape, jnp.float32)
    for kind_id in range(values_table.shape[0]):
        result = jnp.where(material == kind_id, values_table[kind_id], result)
    return result


def paired_terms(own_rows_surface, far_rows_surface, live_rows):
    length_y, length_z = (own_rows_surface.shape[1], own_rows_surface.shape[2])
    group_rows = math.gcd(8, length_y)
    blocks = length_y // group_rows
    own_split = own_rows_surface.reshape(3, blocks, group_rows, length_z).transpose(1, 0, 2, 3)
    far_split = far_rows_surface.reshape(3, blocks, group_rows, length_z).transpose(1, 0, 2, 3)
    live_split = live_rows.reshape(blocks, group_rows)

    def per_block(pieces):
        own_piece, far_piece, live_piece = pieces
        pressure = pair_pressure(own_piece, far_piece)
        return (
            -jnp.sum(pressure, axis=2) * live_piece[:, None],
            -jnp.sum(pressure, axis=1) * live_piece[:, None],
        )

    pushed, reacted = lax.map(per_block, (own_split, far_split, live_split))
    return (pushed.reshape(length_y, length_z), reacted.reshape(length_y, length_z))


def contact_terms(surface, partner_pool, pool_rows, active_part):
    matched = jnp.take(partner_pool, pool_rows, axis=1)
    pushes, reaction = paired_terms(surface, matched, active_part)
    returned = (
        jnp.zeros((partner_pool.shape[1], surface.shape[2]), jnp.float32)
        .at[pool_rows]
        .add(reaction)
    )
    return (pushes, returned)


def spare_terms(surface, partner_pool, pool_rows, active_part):
    return (
        jnp.zeros((surface.shape[1], surface.shape[2]), jnp.float32),
        jnp.zeros((partner_pool.shape[1], surface.shape[2]), jnp.float32),
    )


def local(displacement, velocity, material, moduli, density, partner, active):
    length_x, length_y, length_z = (
        displacement.shape[2],
        displacement.shape[3],
        displacement.shape[4],
    )
    count_x = lax.axis_size("gx")
    count_y = lax.axis_size("yz")
    place_x = lax.axis_index("gx")
    place_y = lax.axis_index("yz")
    place_body = lax.axis_index("body")
    rows_all = length_y * count_y
    whole_x = place_x * length_x + jnp.arange(length_x)
    whole_y = place_y * length_y + jnp.arange(length_y)
    inside = (
        (whole_x < length_x * count_x - 1)[:, None, None]
        & (whole_y < rows_all - 1)[None, :, None]
        & (jnp.arange(length_z) < length_z - 1)[None, None, :]
    )
    elements = jnp.where(inside[None], lookup(material, moduli), 0.0)
    node_mass = lookup(material, density)[:, None]
    shifted = jnp.concatenate([jnp.zeros_like(elements[..., :1]), elements[..., :-1]], axis=3)
    paired = jnp.concatenate([elements, elements + shifted], axis=0)
    below_x = passed_along(paired[:, length_x - 1 :], "gx", 1)
    extended = jnp.concatenate([below_x, paired], axis=1)
    below_y = passed_along(extended[:, :, length_y - 1 :], "yz", 1)
    stiff_halo = jnp.concatenate([below_y, extended], axis=2)
    single = stiff_halo[0]
    summed = stiff_halo[1]
    stiff_x = 0.25 * (summed[: length_x + 1, 1 : length_y + 1] + summed[: length_x + 1, :length_y])
    stiff_y = 0.25 * (summed[1 : length_x + 1, : length_y + 1] + summed[:length_x, : length_y + 1])
    stiff_z = 0.25 * (
        single[1 : length_x + 1, 1 : length_y + 1]
        + single[:length_x, 1 : length_y + 1]
        + single[1 : length_x + 1, :length_y]
        + single[:length_x, :length_y]
    )
    own_rows = lax.dynamic_slice_in_dim(partner, place_y * length_y, length_y)
    active_part = lax.dynamic_slice_in_dim(active, place_y * length_y, length_y).astype(jnp.float32)
    is_face = place_x == count_x - 1
    is_contact = (place_body == 0) & is_face
    pool_rows = (own_rows - place_y * length_y) % rows_all
    for repeat in range(STEPS):
        widened = padded(displacement, (("gx", 2), ("yz", 3)), 1)
        surface = displacement[0, :, length_x - 1]
        pull_x = stiff_x * tension(widened[:, :, 1:, 1:-1] - widened[:, :, :-1, 1:-1])
        forces = pull_x[:, :, 1:] - pull_x[:, :, :-1]
        pull_y = stiff_y * tension(widened[:, :, 1:-1, 1:] - widened[:, :, 1:-1, :-1])
        forces = forces + (pull_y[:, :, :, 1:] - pull_y[:, :, :, :-1])
        forces = forces + axis_forces(displacement, stiff_z, 4)
        across = passed_along(surface, "body", -1)
        onward = shifted_2(across, "yz", -1)
        partner_pool = jnp.concatenate([across, onward], axis=1)
        pushes, returned = lax.cond(
            is_contact, contact_terms, spare_terms, surface, partner_pool, pool_rows, active_part
        )
        carried = shifted_2(returned[length_y:], "yz", 1)
        arriving = passed_along(returned[:length_y] + carried, "body", 1)
        contact = pushes + arriving
        forces = forces.at[0, 0, length_x - 1].add(contact)
        velocity = velocity + STEP_TIME * forces / node_mass
        displacement = displacement + STEP_TIME * velocity
    return (displacement, velocity)


def solution(mesh):
    in_specs = (
        P("body", None, "gx", "yz", None),
        P("body", None, "gx", "yz", None),
        P("body", "gx", "yz", None),
        P(),
        P(),
        P(),
        P(),
    )
    out_specs = (P("body", None, "gx", "yz", None), P("body", None, "gx", "yz", None))
    return jax.shard_map(local, mesh=mesh, in_specs=in_specs, out_specs=out_specs, check_vma=False)
```

profile of v0, /device:TPU:249, one launch (start us, length us, event | category | flops | bytes accessed | tf_op | source)
XLA Modules:
  0.0 183.8 jit_solution(16346014545641997496)
XLA Ops:
  0.7 1.6 fusion.95
  2.4 6.9 %select_select_fusion = (f32[1,16,64,128]{3,2,1,0:T(8,128)S(1)}, pred[1,16,64,128]{3,2,1,0:T(8,128)(4,1)S(1)}, pred[1,16,64,128]{3,2,1,0:T(8,128)(4,1)S(1)}, pre...) fusion(f32[]{:T(128)} %bitcast.87, f32[]{:T(128)} %bitcast.86, ...), kind=kLoop, calls=%fused_computation.222 | loop fusion | flops 2359296 | bytes 2098336 | tf_op jit(solution)/shard_map/jit(_where)/select_n | solution.py:133
  9.5 1.4 collective-permute-start.2
  11.0 1.3 collective-permute-start.1
  12.3 4.6 %collective-permute-start = (f32[1,3,1,64,128]{4,3,2,1,0:T(8,128)S(1)}, f32[1,3,1,64,128]{4,3,2,1,0:T(8,128)S(1)}, u32[]{:S(2)}, u32[]{:S(2)}) collective-permute-start(f32[1,3,1,64,128]{4,3,2,1,0:T(8,128)S(1)} %get-tuple-element.455), channel_id=1, source_target_pairs={{4,0},{8,4},{12,8},{16,12},{20,16},{24,20},{28,24},{32,28},{36,32}... | collective-permute-start | bytes 294920 | tf_op jit(solution)/shard_map/ppermute | solution.py:32
  16.9 1.3 collective-permute-start.6
  18.9 6.3 %select_bitcast_fusion.4 = f32[16,64,128]{2,1,0:T(8,128)} fusion(pred[1,16,64,128]{3,2,1,0:T(8,128)(4,1)S(1)} %get-tuple-element.395, pred[1,16,64,128]{3,2,1,0:T(8,128)(4,1)S(1)} %get-tuple-element.394, pred[1,16,64,128]{3,2,1,0:T(8,128)(4,1)S(1)} %get-tuple-element.393, pred[1,16,64,128]{3,2,1,0:T(8,128)(4,1)S(1)} %get-tuple-element.392, ...), kind=kLoop, calls=%fused_computation.220 | loop fusion | flops 1048576 | bytes 1572896 | tf_op jit(solution)/shard_map/div | solution.py:174
  25.2 4.2 %collective-permute-start.3 = (f32[2,17,1,128]{3,2,1,0:T(1,128)S(1)}, f32[2,17,1,128]{3,2,1,0:T(1,128)S(1)}, u32[]{:S(2)}, u32[]{:S(2)}) collective-permute-start(f32[2,17,1,128]{3,2,1,0:T(1,128)S(1)} %pad_maximum_fusion.34), channel_id=1, source_target_pairs={{0,1},{1,2},{2,3},{4,5},{5,6},{6,7},{8,9},{9,10},{10,11},{12,13},{... | collective-permute-start | bytes 52232 | tf_op jit(solution)/shard_map/ppermute | solution.py:21
  29.5 1.6 slice.551
  31.7 1.8 copy-done.33
  33.4 1.6 tanh_multiply_fusion.3
  35.1 1.9 %collective-permute-start.4 = (f32[1,3,18,1,128]{4,3,2,1,0:T(1,128)S(1)}, f32[1,3,18,1,128]{4,3,2,1,0:T(1,128)S(1)}, u32[]{:S(2)}, u32[]{:S(2)}) collective-permute-start(f32[1,3,18,1,128]{4,3,2,1,0:T(1,128)S(1)} %get-tuple-element.442), channel_id=1, source_target_pairs={{1,0},{2,1},{3,2},{5,4},{6,5},{7,6},{9,8},{10,9},{11,10},{13,12},{... | collective-permute-start | bytes 82952 | tf_op jit(solution)/shard_map/ppermute | solution.py:32
  37.1 3.6 %collective-permute-start.5 = (f32[1,3,18,1,128]{4,3,2,1,0:T(1,128)S(1)}, f32[1,3,18,1,128]{4,3,2,1,0:T(1,128)S(1)}, u32[]{:S(2)}, u32[]{:S(2)}) collective-permute-start(f32[1,3,18,1,128]{4,3,2,1,0:T(1,128)S(1)} %get-tuple-element.443), channel_id=1, source_target_pairs={{0,1},{1,2},{2,3},{4,5},{5,6},{6,7},{8,9},{9,10},{10,11},{12,13},{... | collective-permute-start | bytes 82952 | tf_op jit(solution)/shard_map/ppermute | solution.py:29
  40.8 1.5 fusion.66
  42.3 2.6 %collective-permute-done.7 = f32[3,64,128]{2,1,0:T(8,128)S(1)} collective-permute-done((f32[3,64,128]{2,1,0:T(8,128)S(1)}, f32[3,64,128]{2,1,0:T(8,128)S(1)}, u32[]{:S(2)}, u32[]{:S(2)}) %collective-permute-start.7) | collective-permute-done | bytes 98336 | tf_op jit(solution)/shard_map/ppermute | solution.py:40
  44.9 13.2 %conditional.4 = (f32[64,128]{1,0:T(8,128)}, f32[128,128]{1,0:T(8,128)S(1)}) conditional(s32[]{:T(128)} %convert_element_type.45, () %tuple.73, (f32[1,3,1,64,128]{4,3,2,1,0:T(8,128)S(1)}, f32[3,128,128]{2,1,0:T(8,128)S(1)}, s32[64]{0:T(128)S(1)}, f32[64]{0:T(128)S(1)}) %tuple.74), branch_computations={%region_0.1_spmd, %region_1.8_spmd} | conditional | flops 2661058 | bytes 1237097 | solution.py:167
  46.0 11.3 %while.48 = (s32[]{:T(128)}, f32[8,8,128]{2,1,0:T(8,128)}, f32[8,8,128]{2,1,0:T(8,128)S(1)}, f32[8,3,8,128]{3,2,0,1:T(8,128)S(1)}, f32[8,3,8,128]{3,2,0,1:T(8,128)S(1)}, /*index=5*/f32[8,8]{1,0:T(8,128)S(1)}, s32[]{:T(128)}) while((s32[]{:T(128)}, f32[8,8,128]{2,1,0:T(8,128)}, f32[8,8,128]{2,1,0:T(8,128)S(1)}, f32[8,3,8,128]{3,2,0,1:T(8,128)S(1)}, ...), condition=%wide.region_5.6_spmd, body=%wide.region_2.5_spmd.sunk | while | flops 2626690 | bytes 149653 | solution.py:92
  57.3 0.8 scatter_custom_fusion
  58.3 2.4 %fusion.63 = f32[1,3,16,65,128]{4,3,2,1,0:T(8,128)S(1)} fusion(f32[1,3,18,64,128]{4,3,2,1,0:T(8,128)} %copy-done.34, f32[1,3,18,1,128]{4,3,2,1,0:T(1,128)S(1)} %collective-permute-done.5, f32[1,3,18,1,128]{4,3,2,1,0:T(1,128)S(1)} %collective-permute-done.4, f32[16,65,128]{2,1,0:T(8,128)S(1)} %fusion.85), kind=kLoop, calls=%fused_computation.162 | loop fusion | flops 1996800 | bytes 3954688 | tf_op jit(solution)/shard_map/mul | solution.py:161
  60.7 1.3 collective-permute-start.9
  65.4 1.3 collective-permute-start.14
  66.7 1.3 collective-permute-start.10
  68.0 1.3 collective-permute-start.11
  69.4 1.5 tanh_multiply_fusion.2
  70.9 2.8 %collective-permute-done.11 = f32[1,3,1,64,128]{4,3,2,1,0:T(8,128)S(1)} collective-permute-done((f32[1,3,1,64,128]{4,3,2,1,0:T(8,128)S(1)}, f32[1,3,1,64,128]{4,3,2,1,0:T(8,128)S(1)}, u32[]{:S(2)}, u32[]{:S(2)}) %collective-permute-start.11) | collective-permute-done | bytes 98336 | tf_op jit(solution)/shard_map/ppermute | solution.py:29
  73.7 3.7 %collective-permute-start.12 = (f32[1,3,18,1,128]{4,3,2,1,0:T(1,128)S(1)}, f32[1,3,18,1,128]{4,3,2,1,0:T(1,128)S(1)}, u32[]{:S(2)}, u32[]{:S(2)}) collective-permute-start(f32[1,3,18,1,128]{4,3,2,1,0:T(1,128)S(1)} %get-tuple-element.440), channel_id=1, source_target_pairs={{1,0},{2,1},{3,2},{5,4},{6,5},{7,6},{9,8},{10,9},{11,10},{13,12},{... | collective-permute-start | bytes 82952 | tf_op jit(solution)/shard_map/ppermute | solution.py:32
  77.4 2.4 %collective-permute-start.13 = (f32[1,3,18,1,128]{4,3,2,1,0:T(1,128)S(1)}, f32[1,3,18,1,128]{4,3,2,1,0:T(1,128)S(1)}, u32[]{:S(2)}, u32[]{:S(2)}) collective-permute-start(f32[1,3,18,1,128]{4,3,2,1,0:T(1,128)S(1)} %get-tuple-element.441), channel_id=1, source_target_pairs={{0,1},{1,2},{2,3},{4,5},{5,6},{6,7},{8,9},{9,10},{10,11},{12,13},{... | collective-permute-start | bytes 82952 | tf_op jit(solution)/shard_map/ppermute | solution.py:29
  80.0 1.4 fusion.69
  81.4 2.6 %collective-permute-done.15 = f32[3,64,128]{2,1,0:T(8,128)S(1)} collective-permute-done((f32[3,64,128]{2,1,0:T(8,128)S(1)}, f32[3,64,128]{2,1,0:T(8,128)S(1)}, u32[]{:S(2)}, u32[]{:S(2)}) %collective-permute-start.15) | collective-permute-done | bytes 98336 | tf_op jit(solution)/shard_map/ppermute | solution.py:40
  84.0 13.4 %conditional.5 = (f32[64,128]{1,0:T(8,128)}, f32[128,128]{1,0:T(8,128)S(1)}) conditional(s32[]{:T(128)} %convert_element_type.45, () %tuple.75, (f32[1,3,1,64,128]{4,3,2,1,0:T(8,128)S(1)}, f32[3,128,128]{2,1,0:T(8,128)S(1)}, s32[64]{0:T(128)S(1)}, f32[64]{0:T(128)S(1)}) %tuple.76), branch_computations={%region_7.9_spmd, %region_8.15_spmd} | conditional | flops 2661058 | bytes 1237097 | solution.py:167
  85.1 11.3 %while.49 = (s32[]{:T(128)}, f32[8,8,128]{2,1,0:T(8,128)}, f32[8,8,128]{2,1,0:T(8,128)S(1)}, f32[8,3,8,128]{3,2,0,1:T(8,128)S(1)}, f32[8,3,8,128]{3,2,0,1:T(8,128)S(1)}, /*index=5*/f32[8,8]{1,0:T(8,128)S(1)}, s32[]{:T(128)}) while((s32[]{:T(128)}, f32[8,8,128]{2,1,0:T(8,128)}, f32[8,8,128]{2,1,0:T(8,128)S(1)}, ...), condition=%wide.region_12.13_spmd, body=%wide.region_9.12_spmd.sunk | while | flops 2626690 | bytes 149653 | solution.py:92
  96.4 0.8 scatter_custom_fusion.1
  98.7 1.3 collective-permute-start.17
  101.0 0.9 fusion.90
  102.1 2.0 %multiply_add_fusion.2 = (f32[1,3,16,64,128]{4,3,2,1,0:T(8,128)S(1)}, f32[1,3,16,64,128]{4,3,2,1,0:T(8,128)}) fusion(f32[1,3,16,64,128]{4,3,2,1,0:T(8,128)S(1)} %multiply_add_fusion.3, f32[1,3,16,64,128]{4,3,2,1,0:T(8,128)S(1)} %fusion.90, f32[1,3,16,64,128]{4,3,2,1,0:T(8,128)S(1)} %copy-done.32, f32[16,64,128]{2,1,0:T(8,128)S(1)} %copy-done.28, ...), kind=kLoop, calls=%fused_computation.202 | loop fusion | flops 3145728 | bytes 9961472 | tf_op jit(solution)/shard_map/add | solution.py:175
  104.6 1.3 collective-permute-start.22
  105.9 1.3 collective-permute-start.18
  107.2 1.3 collective-permute-start.19
  108.5 1.5 tanh_multiply_fusion.1
  110.0 2.8 %collective-permute-done.19 = f32[1,3,1,64,128]{4,3,2,1,0:T(8,128)S(1)} collective-permute-done((f32[1,3,1,64,128]{4,3,2,1,0:T(8,128)S(1)}, f32[1,3,1,64,128]{4,3,2,1,0:T(8,128)S(1)}, u32[]{:S(2)}, u32[]{:S(2)}) %collective-permute-start.19) | collective-permute-done | bytes 98336 | tf_op jit(solution)/shard_map/ppermute | solution.py:29
  112.9 3.5 %collective-permute-start.20 = (f32[1,3,18,1,128]{4,3,2,1,0:T(1,128)S(1)}, f32[1,3,18,1,128]{4,3,2,1,0:T(1,128)S(1)}, u32[]{:S(2)}, u32[]{:S(2)}) collective-permute-start(f32[1,3,18,1,128]{4,3,2,1,0:T(1,128)S(1)} %get-tuple-element.438), channel_id=1, source_target_pairs={{1,0},{2,1},{3,2},{5,4},{6,5},{7,6},{9,8},{10,9},{11,10},{13,12},{... | collective-permute-start | bytes 82952 | tf_op jit(solution)/shard_map/ppermute | solution.py:32
  116.4 3.7 %collective-permute-start.21 = (f32[1,3,18,1,128]{4,3,2,1,0:T(1,128)S(1)}, f32[1,3,18,1,128]{4,3,2,1,0:T(1,128)S(1)}, u32[]{:S(2)}, u32[]{:S(2)}) collective-permute-start(f32[1,3,18,1,128]{4,3,2,1,0:T(1,128)S(1)} %get-tuple-element.439), channel_id=1, source_target_pairs={{0,1},{1,2},{2,3},{4,5},{5,6},{6,7},{8,9},{9,10},{10,11},{12,13},{... | collective-permute-start | bytes 82952 | tf_op jit(solution)/shard_map/ppermute | solution.py:29
  120.1 1.4 fusion.72
  121.6 2.6 %collective-permute-done.23 = f32[3,64,128]{2,1,0:T(8,128)S(1)} collective-permute-done((f32[3,64,128]{2,1,0:T(8,128)S(1)}, f32[3,64,128]{2,1,0:T(8,128)S(1)}, u32[]{:S(2)}, u32[]{:S(2)}) %collective-permute-start.23) | collective-permute-done | bytes 98336 | tf_op jit(solution)/shard_map/ppermute | solution.py:40
  124.2 13.2 %conditional.6 = (f32[64,128]{1,0:T(8,128)}, f32[128,128]{1,0:T(8,128)S(1)}) conditional(s32[]{:T(128)} %convert_element_type.45, () %tuple.77, (f32[1,3,1,64,128]{4,3,2,1,0:T(8,128)S(1)}, f32[3,128,128]{2,1,0:T(8,128)S(1)}, s32[64]{0:T(128)S(1)}, f32[64]{0:T(128)S(1)}) %tuple.78), branch_computations={%region_14.16_spmd, %region_15.22_spmd} | conditional | flops 2661058 | bytes 1237097 | solution.py:167
  125.3 11.3 %while.50 = (s32[]{:T(128)}, f32[8,8,128]{2,1,0:T(8,128)}, f32[8,8,128]{2,1,0:T(8,128)S(1)}, f32[8,3,8,128]{3,2,0,1:T(8,128)S(1)}, f32[8,3,8,128]{3,2,0,1:T(8,128)S(1)}, /*index=5*/f32[8,8]{1,0:T(8,128)S(1)}, s32[]{:T(128)}) while((s32[]{:T(128)}, f32[8,8,128]{2,1,0:T(8,128)}, f32[8,8,128]{2,1,0:T(8,128)S(1)}, ...), condition=%wide.region_19.20_spmd, body=%wide.region_16.19_spmd.sunk | while | flops 2626690 | bytes 149653 | solution.py:92
  136.6 0.8 scatter_custom_fusion.2
  138.7 1.3 collective-permute-start.25
  143.4 1.3 collective-permute-start.30
  144.7 1.3 collective-permute-start.26
  146.0 1.3 collective-permute-start.27
  147.3 1.5 tanh_multiply_fusion
  148.9 2.8 %collective-permute-done.27 = f32[1,3,1,64,128]{4,3,2,1,0:T(8,128)S(1)} collective-permute-done((f32[1,3,1,64,128]{4,3,2,1,0:T(8,128)S(1)}, f32[1,3,1,64,128]{4,3,2,1,0:T(8,128)S(1)}, u32[]{:S(2)}, u32[]{:S(2)}) %collective-permute-start.27) | collective-permute-done | bytes 98336 | tf_op jit(solution)/shard_map/ppermute | solution.py:29
  151.7 3.7 %collective-permute-start.28 = (f32[1,3,18,1,128]{4,3,2,1,0:T(1,128)S(1)}, f32[1,3,18,1,128]{4,3,2,1,0:T(1,128)S(1)}, u32[]{:S(2)}, u32[]{:S(2)}) collective-permute-start(f32[1,3,18,1,128]{4,3,2,1,0:T(1,128)S(1)} %get-tuple-element.436), channel_id=1, source_target_pairs={{1,0},{2,1},{3,2},{5,4},{6,5},{7,6},{9,8},{10,9},{11,10},{13,12},{... | collective-permute-start | bytes 82952 | tf_op jit(solution)/shard_map/ppermute | solution.py:32
  155.5 3.7 %collective-permute-start.29 = (f32[1,3,18,1,128]{4,3,2,1,0:T(1,128)S(1)}, f32[1,3,18,1,128]{4,3,2,1,0:T(1,128)S(1)}, u32[]{:S(2)}, u32[]{:S(2)}) collective-permute-start(f32[1,3,18,1,128]{4,3,2,1,0:T(1,128)S(1)} %get-tuple-element.437), channel_id=1, source_target_pairs={{0,1},{1,2},{2,3},{4,5},{5,6},{6,7},{8,9},{9,10},{10,11},{12,13},{... | collective-permute-start | bytes 82952 | tf_op jit(solution)/shard_map/ppermute | solution.py:29
  159.3 1.4 fusion.75
  160.7 2.6 %collective-permute-done.31 = f32[3,64,128]{2,1,0:T(8,128)S(1)} collective-permute-done((f32[3,64,128]{2,1,0:T(8,128)S(1)}, f32[3,64,128]{2,1,0:T(8,128)S(1)}, u32[]{:S(2)}, u32[]{:S(2)}) %collective-permute-start.31) | collective-permute-done | bytes 98336 | tf_op jit(solution)/shard_map/ppermute | solution.py:40
  163.3 13.4 %conditional.7 = (f32[64,128]{1,0:T(8,128)}, f32[128,128]{1,0:T(8,128)S(1)}) conditional(s32[]{:T(128)} %convert_element_type.45, () %tuple.79, (f32[1,3,1,64,128]{4,3,2,1,0:T(8,128)S(1)}, f32[3,128,128]{2,1,0:T(8,128)S(1)}, s32[64]{0:T(128)S(1)}, f32[64]{0:T(128)S(1)}) %tuple.80), branch_computations={%region_21.23_spmd, %region_22.29_spmd} | conditional | flops 2661058 | bytes 1237097 | solution.py:167
  164.4 11.3 %while.51 = (s32[]{:T(128)}, f32[8,8,128]{2,1,0:T(8,128)}, f32[8,8,128]{2,1,0:T(8,128)S(1)}, f32[8,3,8,128]{3,2,0,1:T(8,128)S(1)}, f32[8,3,8,128]{3,2,0,1:T(8,128)S(1)}, /*index=5*/f32[8,8]{1,0:T(8,128)S(1)}, s32[]{:T(128)}) while((s32[]{:T(128)}, f32[8,8,128]{2,1,0:T(8,128)}, f32[8,8,128]{2,1,0:T(8,128)S(1)}, ...), condition=%wide.region_26.27_spmd, body=%wide.region_23.26_spmd.sunk | while | flops 2626690 | bytes 149653 | solution.py:92
  175.7 0.8 scatter_custom_fusion.3
  177.3 0.8 collective-permute-done.32
  178.1 1.3 collective-permute-start.33
  180.4 0.9 fusion.88
  181.4 2.5 %multiply_add_fusion = (f32[1,3,16,64,128]{4,3,2,1,0:T(8,128)}, f32[1,3,16,64,128]{4,3,2,1,0:T(8,128)}) fusion(f32[1,3,16,64,128]{4,3,2,1,0:T(8,128)S(1)} %multiply_add_fusion.1, f32[1,3,16,64,128]{4,3,2,1,0:T(8,128)S(1)} %fusion.88, f32[1,3,16,64,128]{4,3,2,1,0:T(8,128)S(1)} %copy-done.10, f32[16,64,128]{2,1,0:T(8,128)S(1)} %copy-done.30, ...), kind=kLoop, calls=%fused_computation.196 | loop fusion | flops 3145728 | bytes 9961472 | tf_op jit(solution)/shard_map/add | solution.py:175
  (455 shorter events, 62.9 us)
Async XLA Ops:
  9.2 9.0 %copy-start.35 = (f32[8]{0:T(128)S(1)}, f32[8]{0:T(128)}, u32[]{:S(2)}) copy-start(f32[8]{0:T(128)} %param.37) | copy-start | bytes 100
  9.5 19.9 %copy-start.36 = (s32[256]{0:T(256)S(1)}, s32[256]{0:T(256)}, u32[]{:S(2)}) copy-start(s32[256]{0:T(256)} %param.38) | copy-start | bytes 3076
  9.5 19.9 %copy-start.37 = (s32[256]{0:T(256)S(1)}, s32[256]{0:T(256)}, u32[]{:S(2)}) copy-start(s32[256]{0:T(256)} %param.39) | copy-start | bytes 3076
  9.5 15.6 %collective-permute-start.2 = (f32[2,1,64,128]{3,2,1,0:T(8,128)S(1)}, f32[2,1,64,128]{3,2,1,0:T(8,128)S(1)}, u32[]{:S(2)}, u32[]{:S(2)}) collective-permute-start(f32[2,1,64,128]{3,2,1,0:T(8,128)S(1)} %pad_maximum_fusion.24), channel_id=1, source_target_pairs={{0,4},{4,8},{8,12},{12,16},{16,20},{20,24},{24,28},{28,32},{32,36}... | collective-permute-start | bytes 196616 | tf_op jit(solution)/shard_map/ppermute | solution.py:21
  11.0 20.7 %collective-permute-start.1 = (f32[1,3,1,64,128]{4,3,2,1,0:T(8,128)S(1)}, f32[1,3,1,64,128]{4,3,2,1,0:T(8,128)S(1)}, u32[]{:S(2)}, u32[]{:S(2)}) collective-permute-start(f32[1,3,1,64,128]{4,3,2,1,0:T(8,128)S(1)} %get-tuple-element.454), channel_id=1, source_target_pairs={{0,4},{4,8},{8,12},{12,16},{16,20},{20,24},{24,28},{28,32},{32,36}... | collective-permute-start | bytes 294920 | tf_op jit(solution)/shard_map/ppermute | solution.py:29
  12.3 22.8 %collective-permute-start = (f32[1,3,1,64,128]{4,3,2,1,0:T(8,128)S(1)}, f32[1,3,1,64,128]{4,3,2,1,0:T(8,128)S(1)}, u32[]{:S(2)}, u32[]{:S(2)}) collective-permute-start(f32[1,3,1,64,128]{4,3,2,1,0:T(8,128)S(1)} %get-tuple-element.455), channel_id=1, source_target_pairs={{4,0},{8,4},{12,8},{16,12},{20,16},{24,20},{28,24},{32,28},{36,32}... | collective-permute-start | bytes 294920 | tf_op jit(solution)/shard_map/ppermute | solution.py:32
  16.9 23.8 %collective-permute-start.6 = (f32[3,64,128]{2,1,0:T(8,128)S(1)}, f32[3,64,128]{2,1,0:T(8,128)S(1)}, u32[]{:S(2)}, u32[]{:S(2)}) collective-permute-start(f32[3,64,128]{2,1,0:T(8,128)S(1)} %get-tuple-element.453), channel_id=1, source_target_pairs={{128,0},{129,1},{130,2},{131,3},{132,4},{133,5},{134,6},{135,7},{1... | collective-permute-start | bytes 294920 | tf_op jit(solution)/shard_map/ppermute | solution.py:21
  25.2 6.0 %collective-permute-start.3 = (f32[2,17,1,128]{3,2,1,0:T(1,128)S(1)}, f32[2,17,1,128]{3,2,1,0:T(1,128)S(1)}, u32[]{:S(2)}, u32[]{:S(2)}) collective-permute-start(f32[2,17,1,128]{3,2,1,0:T(1,128)S(1)} %pad_maximum_fusion.34), channel_id=1, source_target_pairs={{0,1},{1,2},{2,3},{4,5},{5,6},{6,7},{8,9},{9,10},{10,11},{12,13},{... | collective-permute-start | bytes 52232 | tf_op jit(solution)/shard_map/ppermute | solution.py:21
  31.4 26.8 %copy-start.1 = (f32[16,65,128]{2,1,0:T(8,128)}, f32[16,65,128]{2,1,0:T(8,128)S(1)}, u32[]{:S(2)}) copy-start(f32[16,65,128]{2,1,0:T(8,128)S(1)} %fusion.85) | copy-start | bytes 1597444
  31.5 9.3 %copy-start.15 = (f32[17,64,128]{2,1,0:T(8,128)}, f32[17,64,128]{2,1,0:T(8,128)S(1)}, u32[]{:S(2)}) copy-start(f32[17,64,128]{2,1,0:T(8,128)S(1)} %fusion.86) | copy-start | bytes 1671172
  31.5 1.9 %copy-start.33 = (f32[1,3,16,64,127]{4,3,2,1,0:T(8,128)S(1)}, f32[1,3,16,64,127]{4,3,2,1,0:T(8,128)}, u32[]{:S(2)}) copy-start(f32[1,3,16,64,127]{4,3,2,1,0:T(8,128)} %slice.551) | copy-start | bytes 4681732
  31.6 3.4 %copy-start.23 = (f32[16,64,128]{2,1,0:T(8,128)}, f32[16,64,128]{2,1,0:T(8,128)S(1)}, u32[]{:S(2)}) copy-start(f32[16,64,128]{2,1,0:T(8,128)S(1)} %fusion.87) | copy-start | bytes 1572868
  35.1 7.2 %copy-start.34 = (f32[1,3,18,64,128]{4,3,2,1,0:T(8,128)}, f32[1,3,18,64,128]{4,3,2,1,0:T(8,128)S(1)}, u32[]{:S(2)}) copy-start(f32[1,3,18,64,128]{4,3,2,1,0:T(8,128)S(1)} %constant_dynamic-update-slice_fusion) | copy-start | bytes 5308420
  35.1 23.1 %collective-permute-start.4 = (f32[1,3,18,1,128]{4,3,2,1,0:T(1,128)S(1)}, f32[1,3,18,1,128]{4,3,2,1,0:T(1,128)S(1)}, u32[]{:S(2)}, u32[]{:S(2)}) collective-permute-start(f32[1,3,18,1,128]{4,3,2,1,0:T(1,128)S(1)} %get-tuple-element.442), channel_id=1, source_target_pairs={{1,0},{2,1},{3,2},{5,4},{6,5},{7,6},{9,8},{10,9},{11,10},{13,12},{... | collective-permute-start | bytes 82952 | tf_op jit(solution)/shard_map/ppermute | solution.py:32
  37.1 21.2 %collective-permute-start.5 = (f32[1,3,18,1,128]{4,3,2,1,0:T(1,128)S(1)}, f32[1,3,18,1,128]{4,3,2,1,0:T(1,128)S(1)}, u32[]{:S(2)}, u32[]{:S(2)}) collective-permute-start(f32[1,3,18,1,128]{4,3,2,1,0:T(1,128)S(1)} %get-tuple-element.443), channel_id=1, source_target_pairs={{0,1},{1,2},{2,3},{4,5},{5,6},{6,7},{8,9},{9,10},{10,11},{12,13},{... | collective-permute-start | bytes 82952 | tf_op jit(solution)/shard_map/ppermute | solution.py:29
  40.7 4.1 %collective-permute-start.7 = (f32[3,64,128]{2,1,0:T(8,128)S(1)}, f32[3,64,128]{2,1,0:T(8,128)S(1)}, u32[]{:S(2)}, u32[]{:S(2)}) collective-permute-start(f32[3,64,128]{2,1,0:T(8,128)S(1)} %collective-permute-done.6), channel_id=1, source_target_pairs={{0,3},{1,0},{2,1},{3,2},{4,7},{5,4},{6,5},{7,6},{8,11},{9,8},{10,9... | collective-permute-start | bytes 294920 | tf_op jit(solution)/shard_map/ppermute | solution.py:40
  58.1 3.9 %copy-start.14 = (f32[1,3,16,64,128]{4,3,2,1,0:T(8,128)S(1)}, f32[1,3,16,64,128]{4,3,2,1,0:T(8,128)}, u32[]{:S(2)}) copy-start(f32[1,3,16,64,128]{4,3,2,1,0:T(8,128)} %get-tuple-element.456) | copy-start | bytes 4718596
  58.1 3.9 %copy-start.20 = (f32[1,3,17,64,128]{4,3,2,1,0:T(8,128)S(1)}, f32[1,3,17,64,128]{4,3,2,1,0:T(8,128)}, u32[]{:S(2)}) copy-start(f32[1,3,17,64,128]{4,3,2,1,0:T(8,128)} %fusion.66) | copy-start | bytes 5013508
  58.1 2.5 %collective-permute-start.8 = (f32[64,128]{1,0:T(8,128)S(1)}, f32[64,128]{1,0:T(8,128)S(1)}, u32[]{:S(2)}, u32[]{:S(2)}) collective-permute-start(f32[64,128]{1,0:T(8,128)S(1)} %slice.560), channel_id=1, source_target_pairs={{0,1},{1,2},{2,3},{3,0},{4,5},{5,6},{6,7},{7,4},{8,9},{9,10},{10,1... | collective-permute-start | bytes 98312 | tf_op jit(solution)/shard_map/ppermute | solution.py:40
  60.7 2.3 %collective-permute-start.9 = (f32[64,128]{1,0:T(8,128)S(1)}, f32[64,128]{1,0:T(8,128)S(1)}, u32[]{:S(2)}, u32[]{:S(2)}) collective-permute-start(f32[64,128]{1,0:T(8,128)S(1)} %slice_add_fusion.12), channel_id=1, source_target_pairs={{0,128},{1,129},{2,130},{3,131},{4,132},{5,133},{6,134},{7,135},{8... | collective-permute-start | bytes 98312 | tf_op jit(solution)/shard_map/ppermute | solution.py:21
  65.0 4.4 %copy-start.24 = (f32[16,64,128]{2,1,0:T(8,128)S(1)}, f32[16,64,128]{2,1,0:T(8,128)}, u32[]{:S(2)}) copy-start(f32[16,64,128]{2,1,0:T(8,128)} %copy-done.23) | copy-start | bytes 1572868
  65.4 14.4 %collective-permute-start.14 = (f32[3,64,128]{2,1,0:T(8,128)S(1)}, f32[3,64,128]{2,1,0:T(8,128)S(1)}, u32[]{:S(2)}, u32[]{:S(2)}) collective-permute-start(f32[3,64,128]{2,1,0:T(8,128)S(1)} %get-tuple-element.450), channel_id=1, source_target_pairs={{128,0},{129,1},{130,2},{131,3},{132,4},{133,5},{134,6},{135,7},{1... | collective-permute-start | bytes 294920 | tf_op jit(solution)/shard_map/ppermute | solution.py:21
  66.7 4.2 %collective-permute-start.10 = (f32[1,3,1,64,128]{4,3,2,1,0:T(8,128)S(1)}, f32[1,3,1,64,128]{4,3,2,1,0:T(8,128)S(1)}, u32[]{:S(2)}, u32[]{:S(2)}) collective-permute-start(f32[1,3,1,64,128]{4,3,2,1,0:T(8,128)S(1)} %get-tuple-element.452), channel_id=1, source_target_pairs={{4,0},{8,4},{12,8},{16,12},{20,16},{24,20},{28,24},{32,28},{36,32}... | collective-permute-start | bytes 294920 | tf_op jit(solution)/shard_map/ppermute | solution.py:32
  68.0 5.7 %collective-permute-start.11 = (f32[1,3,1,64,128]{4,3,2,1,0:T(8,128)S(1)}, f32[1,3,1,64,128]{4,3,2,1,0:T(8,128)S(1)}, u32[]{:S(2)}, u32[]{:S(2)}) collective-permute-start(f32[1,3,1,64,128]{4,3,2,1,0:T(8,128)S(1)} %get-tuple-element.451), channel_id=1, source_target_pairs={{0,4},{4,8},{8,12},{12,16},{16,20},{20,24},{24,28},{28,32},{32,36}... | collective-permute-start | bytes 294920 | tf_op jit(solution)/shard_map/ppermute | solution.py:29
  70.9 9.1 %copy-start.16 = (f32[17,64,128]{2,1,0:T(8,128)S(1)}, f32[17,64,128]{2,1,0:T(8,128)}, u32[]{:S(2)}) copy-start(f32[17,64,128]{2,1,0:T(8,128)} %copy-done.15) | copy-start | bytes 1671172
  73.7 23.8 %collective-permute-start.12 = (f32[1,3,18,1,128]{4,3,2,1,0:T(1,128)S(1)}, f32[1,3,18,1,128]{4,3,2,1,0:T(1,128)S(1)}, u32[]{:S(2)}, u32[]{:S(2)}) collective-permute-start(f32[1,3,18,1,128]{4,3,2,1,0:T(1,128)S(1)} %get-tuple-element.440), channel_id=1, source_target_pairs={{1,0},{2,1},{3,2},{5,4},{6,5},{7,6},{9,8},{10,9},{11,10},{13,12},{... | collective-permute-start | bytes 82952 | tf_op jit(solution)/shard_map/ppermute | solution.py:32
  77.4 20.1 %collective-permute-start.13 = (f32[1,3,18,1,128]{4,3,2,1,0:T(1,128)S(1)}, f32[1,3,18,1,128]{4,3,2,1,0:T(1,128)S(1)}, u32[]{:S(2)}, u32[]{:S(2)}) collective-permute-start(f32[1,3,18,1,128]{4,3,2,1,0:T(1,128)S(1)} %get-tuple-element.441), channel_id=1, source_target_pairs={{0,1},{1,2},{2,3},{4,5},{5,6},{6,7},{8,9},{9,10},{10,11},{12,13},{... | collective-permute-start | bytes 82952 | tf_op jit(solution)/shard_map/ppermute | solution.py:29
  79.9 4.1 %collective-permute-start.15 = (f32[3,64,128]{2,1,0:T(8,128)S(1)}, f32[3,64,128]{2,1,0:T(8,128)S(1)}, u32[]{:S(2)}, u32[]{:S(2)}) collective-permute-start(f32[3,64,128]{2,1,0:T(8,128)S(1)} %collective-permute-done.14), channel_id=1, source_target_pairs={{0,3},{1,0},{2,1},{3,2},{4,7},{5,4},{6,5},{7,6},{8,11},{9,8},{10,9... | collective-permute-start | bytes 294920 | tf_op jit(solution)/shard_map/ppermute | solution.py:40
  84.0 13.5 %copy-start.2 = (f32[16,65,128]{2,1,0:T(8,128)S(1)}, f32[16,65,128]{2,1,0:T(8,128)}, u32[]{:S(2)}) copy-start(f32[16,65,128]{2,1,0:T(8,128)} %copy-done.1) | copy-start | bytes 1597444
  97.4 2.6 %copy-start.12 = (f32[1,3,16,64,128]{4,3,2,1,0:T(8,128)S(1)}, f32[1,3,16,64,128]{4,3,2,1,0:T(8,128)}, u32[]{:S(2)}) copy-start(f32[1,3,16,64,128]{4,3,2,1,0:T(8,128)} %tanh_multiply_fusion.2) | copy-start | bytes 4718596
  97.4 2.6 %copy-start.21 = (f32[1,3,17,64,128]{4,3,2,1,0:T(8,128)S(1)}, f32[1,3,17,64,128]{4,3,2,1,0:T(8,128)}, u32[]{:S(2)}) copy-start(f32[1,3,17,64,128]{4,3,2,1,0:T(8,128)} %fusion.69) | copy-start | bytes 5013508
  97.4 1.3 collective-permute-start.16
  98.7 2.3 %collective-permute-start.17 = (f32[64,128]{1,0:T(8,128)S(1)}, f32[64,128]{1,0:T(8,128)S(1)}, u32[]{:S(2)}, u32[]{:S(2)}) collective-permute-start(f32[64,128]{1,0:T(8,128)S(1)} %slice_add_fusion.11), channel_id=1, source_target_pairs={{0,128},{1,129},{2,130},{3,131},{4,132},{5,133},{6,134},{7,135},{8... | collective-permute-start | bytes 98312 | tf_op jit(solution)/shard_map/ppermute | solution.py:21
  100.0 1.9 %copy-start.6 = (f32[1,3,16,64,128]{4,3,2,1,0:T(8,128)S(1)}, f32[1,3,16,64,128]{4,3,2,1,0:T(8,128)}, u32[]{:S(2)}) copy-start(f32[1,3,16,64,128]{4,3,2,1,0:T(8,128)} %copy-done.5) | copy-start | bytes 4718596
  100.1 2.0 %copy-start.32 = (f32[1,3,16,64,128]{4,3,2,1,0:T(8,128)S(1)}, f32[1,3,16,64,128]{4,3,2,1,0:T(8,128)}, u32[]{:S(2)}) copy-start(f32[1,3,16,64,128]{4,3,2,1,0:T(8,128)} %param.34) | copy-start | bytes 4718596
  104.1 4.4 %copy-start.25 = (f32[16,64,128]{2,1,0:T(8,128)S(1)}, f32[16,64,128]{2,1,0:T(8,128)}, u32[]{:S(2)}) copy-start(f32[16,64,128]{2,1,0:T(8,128)} %copy-done.23) | copy-start | bytes 1572868
  104.6 15.4 %collective-permute-start.22 = (f32[3,64,128]{2,1,0:T(8,128)S(1)}, f32[3,64,128]{2,1,0:T(8,128)S(1)}, u32[]{:S(2)}, u32[]{:S(2)}) collective-permute-start(f32[3,64,128]{2,1,0:T(8,128)S(1)} %get-tuple-element.447), channel_id=1, source_target_pairs={{128,0},{129,1},{130,2},{131,3},{132,4},{133,5},{134,6},{135,7},{1... | collective-permute-start | bytes 294920 | tf_op jit(solution)/shard_map/ppermute | solution.py:21
  105.9 4.2 %collective-permute-start.18 = (f32[1,3,1,64,128]{4,3,2,1,0:T(8,128)S(1)}, f32[1,3,1,64,128]{4,3,2,1,0:T(8,128)S(1)}, u32[]{:S(2)}, u32[]{:S(2)}) collective-permute-start(f32[1,3,1,64,128]{4,3,2,1,0:T(8,128)S(1)} %get-tuple-element.449), channel_id=1, source_target_pairs={{4,0},{8,4},{12,8},{16,12},{20,16},{24,20},{28,24},{32,28},{36,32}... | collective-permute-start | bytes 294920 | tf_op jit(solution)/shard_map/ppermute | solution.py:32
  107.2 5.7 %collective-permute-start.19 = (f32[1,3,1,64,128]{4,3,2,1,0:T(8,128)S(1)}, f32[1,3,1,64,128]{4,3,2,1,0:T(8,128)S(1)}, u32[]{:S(2)}, u32[]{:S(2)}) collective-permute-start(f32[1,3,1,64,128]{4,3,2,1,0:T(8,128)S(1)} %get-tuple-element.448), channel_id=1, source_target_pairs={{0,4},{4,8},{8,12},{12,16},{16,20},{20,24},{24,28},{28,32},{32,36}... | collective-permute-start | bytes 294920 | tf_op jit(solution)/shard_map/ppermute | solution.py:29
  110.0 10.1 %copy-start.17 = (f32[17,64,128]{2,1,0:T(8,128)S(1)}, f32[17,64,128]{2,1,0:T(8,128)}, u32[]{:S(2)}) copy-start(f32[17,64,128]{2,1,0:T(8,128)} %copy-done.15) | copy-start | bytes 1671172
  112.9 24.6 %collective-permute-start.20 = (f32[1,3,18,1,128]{4,3,2,1,0:T(1,128)S(1)}, f32[1,3,18,1,128]{4,3,2,1,0:T(1,128)S(1)}, u32[]{:S(2)}, u32[]{:S(2)}) collective-permute-start(f32[1,3,18,1,128]{4,3,2,1,0:T(1,128)S(1)} %get-tuple-element.438), channel_id=1, source_target_pairs={{1,0},{2,1},{3,2},{5,4},{6,5},{7,6},{9,8},{10,9},{11,10},{13,12},{... | collective-permute-start | bytes 82952 | tf_op jit(solution)/shard_map/ppermute | solution.py:32
  116.4 21.2 %collective-permute-start.21 = (f32[1,3,18,1,128]{4,3,2,1,0:T(1,128)S(1)}, f32[1,3,18,1,128]{4,3,2,1,0:T(1,128)S(1)}, u32[]{:S(2)}, u32[]{:S(2)}) collective-permute-start(f32[1,3,18,1,128]{4,3,2,1,0:T(1,128)S(1)} %get-tuple-element.439), channel_id=1, source_target_pairs={{0,1},{1,2},{2,3},{4,5},{5,6},{6,7},{8,9},{9,10},{10,11},{12,13},{... | collective-permute-start | bytes 82952 | tf_op jit(solution)/shard_map/ppermute | solution.py:29
  120.0 4.1 %collective-permute-start.23 = (f32[3,64,128]{2,1,0:T(8,128)S(1)}, f32[3,64,128]{2,1,0:T(8,128)S(1)}, u32[]{:S(2)}, u32[]{:S(2)}) collective-permute-start(f32[3,64,128]{2,1,0:T(8,128)S(1)} %collective-permute-done.22), channel_id=1, source_target_pairs={{0,3},{1,0},{2,1},{3,2},{4,7},{5,4},{6,5},{7,6},{8,11},{9,8},{10,9... | collective-permute-start | bytes 294920 | tf_op jit(solution)/shard_map/ppermute | solution.py:40
  124.2 13.4 %copy-start.3 = (f32[16,65,128]{2,1,0:T(8,128)S(1)}, f32[16,65,128]{2,1,0:T(8,128)}, u32[]{:S(2)}) copy-start(f32[16,65,128]{2,1,0:T(8,128)} %copy-done.1) | copy-start | bytes 1597444
  137.4 2.6 %copy-start.13 = (f32[1,3,16,64,128]{4,3,2,1,0:T(8,128)S(1)}, f32[1,3,16,64,128]{4,3,2,1,0:T(8,128)}, u32[]{:S(2)}) copy-start(f32[1,3,16,64,128]{4,3,2,1,0:T(8,128)} %tanh_multiply_fusion.1) | copy-start | bytes 4718596
  137.4 2.6 %copy-start.22 = (f32[1,3,17,64,128]{4,3,2,1,0:T(8,128)S(1)}, f32[1,3,17,64,128]{4,3,2,1,0:T(8,128)}, u32[]{:S(2)}) copy-start(f32[1,3,17,64,128]{4,3,2,1,0:T(8,128)} %fusion.72) | copy-start | bytes 5013508
  137.4 1.3 collective-permute-start.24
  138.7 2.3 %collective-permute-start.25 = (f32[64,128]{1,0:T(8,128)S(1)}, f32[64,128]{1,0:T(8,128)S(1)}, u32[]{:S(2)}, u32[]{:S(2)}) collective-permute-start(f32[64,128]{1,0:T(8,128)S(1)} %slice_add_fusion.10), channel_id=1, source_target_pairs={{0,128},{1,129},{2,130},{3,131},{4,132},{5,133},{6,134},{7,135},{8... | collective-permute-start | bytes 98312 | tf_op jit(solution)/shard_map/ppermute | solution.py:21
  142.9 4.4 %copy-start.26 = (f32[16,64,128]{2,1,0:T(8,128)S(1)}, f32[16,64,128]{2,1,0:T(8,128)}, u32[]{:S(2)}) copy-start(f32[16,64,128]{2,1,0:T(8,128)} %copy-done.23) | copy-start | bytes 1572868
  143.4 15.7 %collective-permute-start.30 = (f32[3,64,128]{2,1,0:T(8,128)S(1)}, f32[3,64,128]{2,1,0:T(8,128)S(1)}, u32[]{:S(2)}, u32[]{:S(2)}) collective-permute-start(f32[3,64,128]{2,1,0:T(8,128)S(1)} %get-tuple-element.444), channel_id=1, source_target_pairs={{128,0},{129,1},{130,2},{131,3},{132,4},{133,5},{134,6},{135,7},{1... | collective-permute-start | bytes 294920 | tf_op jit(solution)/shard_map/ppermute | solution.py:21
  144.7 4.2 %collective-permute-start.26 = (f32[1,3,1,64,128]{4,3,2,1,0:T(8,128)S(1)}, f32[1,3,1,64,128]{4,3,2,1,0:T(8,128)S(1)}, u32[]{:S(2)}, u32[]{:S(2)}) collective-permute-start(f32[1,3,1,64,128]{4,3,2,1,0:T(8,128)S(1)} %get-tuple-element.446), channel_id=1, source_target_pairs={{4,0},{8,4},{12,8},{16,12},{20,16},{24,20},{28,24},{32,28},{36,32}... | collective-permute-start | bytes 294920 | tf_op jit(solution)/shard_map/ppermute | solution.py:32
  146.0 5.7 %collective-permute-start.27 = (f32[1,3,1,64,128]{4,3,2,1,0:T(8,128)S(1)}, f32[1,3,1,64,128]{4,3,2,1,0:T(8,128)S(1)}, u32[]{:S(2)}, u32[]{:S(2)}) collective-permute-start(f32[1,3,1,64,128]{4,3,2,1,0:T(8,128)S(1)} %get-tuple-element.445), channel_id=1, source_target_pairs={{0,4},{4,8},{8,12},{12,16},{16,20},{20,24},{24,28},{28,32},{32,36}... | collective-permute-start | bytes 294920 | tf_op jit(solution)/shard_map/ppermute | solution.py:29
  148.9 10.4 %copy-start.18 = (f32[17,64,128]{2,1,0:T(8,128)S(1)}, f32[17,64,128]{2,1,0:T(8,128)}, u32[]{:S(2)}) copy-start(f32[17,64,128]{2,1,0:T(8,128)} %copy-done.15) | copy-start | bytes 1671172
  151.7 25.1 %collective-permute-start.28 = (f32[1,3,18,1,128]{4,3,2,1,0:T(1,128)S(1)}, f32[1,3,18,1,128]{4,3,2,1,0:T(1,128)S(1)}, u32[]{:S(2)}, u32[]{:S(2)}) collective-permute-start(f32[1,3,18,1,128]{4,3,2,1,0:T(1,128)S(1)} %get-tuple-element.436), channel_id=1, source_target_pairs={{1,0},{2,1},{3,2},{5,4},{6,5},{7,6},{9,8},{10,9},{11,10},{13,12},{... | collective-permute-start | bytes 82952 | tf_op jit(solution)/shard_map/ppermute | solution.py:32
  155.5 21.4 %collective-permute-start.29 = (f32[1,3,18,1,128]{4,3,2,1,0:T(1,128)S(1)}, f32[1,3,18,1,128]{4,3,2,1,0:T(1,128)S(1)}, u32[]{:S(2)}, u32[]{:S(2)}) collective-permute-start(f32[1,3,18,1,128]{4,3,2,1,0:T(1,128)S(1)} %get-tuple-element.437), channel_id=1, source_target_pairs={{0,1},{1,2},{2,3},{4,5},{5,6},{6,7},{8,9},{9,10},{10,11},{12,13},{... | collective-permute-start | bytes 82952 | tf_op jit(solution)/shard_map/ppermute | solution.py:29
  159.2 4.1 %collective-permute-start.31 = (f32[3,64,128]{2,1,0:T(8,128)S(1)}, f32[3,64,128]{2,1,0:T(8,128)S(1)}, u32[]{:S(2)}, u32[]{:S(2)}) collective-permute-start(f32[3,64,128]{2,1,0:T(8,128)S(1)} %collective-permute-done.30), channel_id=1, source_target_pairs={{0,3},{1,0},{2,1},{3,2},{4,7},{5,4},{6,5},{7,6},{8,11},{9,8},{10,9... | collective-permute-start | bytes 294920 | tf_op jit(solution)/shard_map/ppermute | solution.py:40
  163.3 13.6 %copy-start.4 = (f32[16,65,128]{2,1,0:T(8,128)S(1)}, f32[16,65,128]{2,1,0:T(8,128)}, u32[]{:S(2)}) copy-start(f32[16,65,128]{2,1,0:T(8,128)} %copy-done.1) | copy-start | bytes 1597444
  176.7 2.6 %copy-start.11 = (f32[1,3,16,64,128]{4,3,2,1,0:T(8,128)S(1)}, f32[1,3,16,64,128]{4,3,2,1,0:T(8,128)}, u32[]{:S(2)}) copy-start(f32[1,3,16,64,128]{4,3,2,1,0:T(8,128)} %tanh_multiply_fusion) | copy-start | bytes 4718596
  176.8 2.6 %copy-start.19 = (f32[1,3,17,64,128]{4,3,2,1,0:T(8,128)S(1)}, f32[1,3,17,64,128]{4,3,2,1,0:T(8,128)}, u32[]{:S(2)}) copy-start(f32[1,3,17,64,128]{4,3,2,1,0:T(8,128)} %fusion.75) | copy-start | bytes 5013508
  176.8 1.3 collective-permute-start.32
  178.1 2.3 %collective-permute-start.33 = (f32[64,128]{1,0:T(8,128)S(1)}, f32[64,128]{1,0:T(8,128)S(1)}, u32[]{:S(2)}, u32[]{:S(2)}) collective-permute-start(f32[64,128]{1,0:T(8,128)S(1)} %slice_add_fusion.9), channel_id=1, source_target_pairs={{0,128},{1,129},{2,130},{3,131},{4,132},{5,133},{6,134},{7,135},{8... | collective-permute-start | bytes 98312 | tf_op jit(solution)/shard_map/ppermute | solution.py:21
  179.4 1.9 %copy-start.8 = (f32[1,3,16,64,128]{4,3,2,1,0:T(8,128)S(1)}, f32[1,3,16,64,128]{4,3,2,1,0:T(8,128)}, u32[]{:S(2)}) copy-start(f32[1,3,16,64,128]{4,3,2,1,0:T(8,128)} %copy-done.7) | copy-start | bytes 4718596
  179.4 1.9 %copy-start.10 = (f32[1,3,16,64,128]{4,3,2,1,0:T(8,128)S(1)}, f32[1,3,16,64,128]{4,3,2,1,0:T(8,128)}, u32[]{:S(2)}) copy-start(f32[1,3,16,64,128]{4,3,2,1,0:T(8,128)} %get-tuple-element.386) | copy-start | bytes 4718596
  179.4 2.0 %copy-start.30 = (f32[16,64,128]{2,1,0:T(8,128)S(1)}, f32[16,64,128]{2,1,0:T(8,128)}, u32[]{:S(2)}) copy-start(f32[16,64,128]{2,1,0:T(8,128)} %select_bitcast_fusion.4) | copy-start | bytes 1572868
  (8 other events, 12.9 us)
where the time goes:
time: 188 us; the launch traced here: 184 us
  other arithmetic  88.7 us (47%)
  starting transfers between devices  56.5 us (30%)
  waiting for transfers between devices  22.2 us (12%)
  local copies, waits for them, and re-layouts  12.9 us (7%)
    reduce_sum x32, other arithmetic, per_block(): jnp.sum(pressure, axis=1)  21.8 us
    dynamic_update_slice x32, other arithmetic, paired_terms(): pushed, reacted = lax.map(per_block, (own_split, far_split, live_split))  21.3 us
    ppermute x8, starting transfers between devices, padded(): lax.ppermute(lax.slice_in_dim(block, 0, width, axis=dim), axis, backward)  21.3 us
    ppermute x8, starting transfers between devices, padded(): lax.ppermute(lax.slice_in_dim(block, block.shape[dim] - width, None, axis...  18.6 us
    ppermute x10, starting transfers between devices, passed_along(): return lax.ppermute(block, axis, route)  16 us
    ppermute x8, waiting for transfers between devices, shifted_2(): return lax.ppermute(value, axis, pairs)  12.7 us
    ppermute x8, waiting for transfers between devices, padded(): lax.ppermute(lax.slice_in_dim(block, block.shape[dim] - width, None, axis...  8.41 us
    select_n x1, other arithmetic, local(): elements = jnp.where(inside[None], lookup(material, moduli), 0.0)  6.85 us
  transfers between devices with their start and end apart: 34, of which 14 were waited for; matrix products, arithmetic and copies ran while one was open for 43% of the time, Pallas kernels for 0%

commit v1 on v0

v1 whole, which is shorter than its diff:
```python
import functools
import math

import jax
import jax.numpy as jnp
from jax import lax
from jax.experimental import pallas as pl
from jax.experimental.pallas import tpu as pltpu
from jax.sharding import PartitionSpec as P

STEPS = 4
STEP_TIME = 0.2
YIELD_SPAN = 0.5
PENALTY = 4.0
SOFT_WIDTH = 0.1
KERNEL_WIDTH = 1.5
LOG2E = 1.0 / math.log(2.0)
PLANE = math.sqrt(LOG2E / (2.0 * KERNEL_WIDTH * KERNEL_WIDTH))
GROUP = 8

MESH = pl.DeviceIdType.MESH
HIGHEST = lax.Precision.HIGHEST


def kernel(
    count_x, count_y, dims,
    disp, velo, mat_hbm, moduli, density, partner, active,
    out_d, out_v,
    D, V, M, E, SX, SY, SYL, SZ, C,
    XH, YH, YS, MX, MY, MC, MYS, CP, G, GT, ACT, WT, FX,
    load_sem, out_sem, m_send, m_recv, x_send, x_recv, y_send, y_recv, c_send, c_recv,
):
    length_x, length_y, length_z = dims
    last = length_x - 1
    body = lax.axis_index("body")
    gx = lax.axis_index("gx")
    yz = lax.axis_index("yz")
    has_lo = gx > 0
    has_hi = gx < count_x - 1
    has_dn = yz > 0
    has_up = yz < count_y - 1
    is_face = gx == count_x - 1
    cross = lax.rem(yz + 1 - 2 * body + count_y, count_y)
    other = 1 - body

    low = {"gx": gx - 1}
    high = {"gx": gx + 1}
    down = {"yz": yz - 1}
    up = {"yz": yz + 1}
    corner_up = {"gx": gx + 1, "yz": yz + 1}
    corner_dn = {"gx": gx - 1, "yz": yz - 1}
    same_peer = {"body": other}
    cross_peer = {"body": other, "yz": cross}

    row_id = lax.broadcasted_iota(jnp.int32, (length_y, length_z), 0)
    lane_id = lax.broadcasted_iota(jnp.int32, (length_y, length_z), 1)

    loads = [
        pltpu.make_async_copy(mat_hbm.at[0], M, load_sem.at[0]),
        pltpu.make_async_copy(disp.at[0], D.at[0], load_sem.at[1]),
        pltpu.make_async_copy(velo.at[0], V, load_sem.at[2]),
    ]
    for item in loads:
        item.start()

    barrier = pltpu.get_barrier_semaphore()

    def greet(condition, device):
        @pl.when(condition)
        def _():
            pl.semaphore_signal(barrier, inc=1, device_id=device, device_id_type=MESH)

    pairs = [
        (has_lo, low), (has_hi, high), (has_dn, down), (has_up, up),
        (has_hi & has_up, corner_up), (has_lo & has_dn, corner_dn),
        (is_face, same_peer), (is_face, cross_peer),
    ]
    for condition, device in pairs:
        greet(condition, device)
    pl.semaphore_wait(barrier, sum(condition.astype(jnp.int32) for condition, _ in pairs))

    def remote(source, target, send, recv, device):
        return pltpu.make_async_remote_copy(
            src_ref=source, dst_ref=target, send_sem=send, recv_sem=recv,
            device_id=device, device_id_type=MESH,
        )

    def x_up(s, source):
        return remote(source, XH.at[s, 0], x_send.at[s, 0], x_recv.at[s, 0], high)

    def x_down(s, source):
        return remote(source, XH.at[s, 1], x_send.at[s, 1], x_recv.at[s, 1], low)

    def y_up(s):
        return remote(YS.at[s, 0], YH.at[s, 0], y_send.at[s, 0], y_recv.at[s, 0], up)

    def y_down(s):
        return remote(YS.at[s, 1], YH.at[s, 1], y_send.at[s, 1], y_recv.at[s, 1], down)

    def c_same(s, c, source):
        return remote(source, CP.at[s, c, 0], c_send.at[s, c, 0], c_recv.at[s, c, 0], same_peer)

    def c_cross(s, c, source):
        return remote(source, CP.at[s, c, 1], c_send.at[s, c, 1], c_recv.at[s, c, 1], cross_peer)

    m_x = remote(mat_hbm.at[0, last], MX, m_send.at[0], m_recv.at[0], high)
    m_y = remote(MYS, MY, m_send.at[1], m_recv.at[1], up)
    m_c = remote(MYS.at[pl.ds(length_x - 8, 8)], MC, m_send.at[2], m_recv.at[2], corner_up)

    @pl.when(has_hi)
    def _():
        m_x.start()
        x_up(0, disp.at[0, :, last]).start()

    @pl.when(has_lo)
    def _():
        x_down(0, disp.at[0, :, 0]).start()

    @pl.when(is_face)
    def _():
        for c in (1, 2, 0):
            c_same(0, c, disp.at[0, c, last]).start()
            c_cross(0, c, disp.at[0, c, last]).start()

    @pl.when(jnp.logical_not(has_lo))
    def _():
        XH[:, 0] = jnp.zeros((STEPS, 3, length_y, length_z), jnp.float32)

    @pl.when(jnp.logical_not(has_hi))
    def _():
        XH[:, 1] = jnp.zeros((STEPS, 3, length_y, length_z), jnp.float32)

    @pl.when(jnp.logical_not(has_dn))
    def _():
        YH[:, 0] = jnp.zeros((STEPS, 3, length_x, length_z), jnp.float32)
        MY[...] = jnp.zeros((length_x, length_z), jnp.int32)

    @pl.when(jnp.logical_not(has_up))
    def _():
        YH[:, 1] = jnp.zeros((STEPS, 3, length_x, length_z), jnp.float32)

    @pl.when(jnp.logical_not(has_lo))
    def _():
        MX[...] = jnp.zeros((length_y, length_z), jnp.int32)

    @pl.when(jnp.logical_not(has_lo & has_dn))
    def _():
        MC[...] = jnp.zeros((8, length_z), jnp.int32)

    loads[0].wait()

    @pl.loop(0, length_x)
    def _(i):
        MYS[pl.ds(i, 1)] = M[i, pl.ds(length_y - 1, 1)]

    @pl.when(has_up)
    def _():
        m_y.start()

    @pl.when(has_hi & has_up)
    def _():
        m_c.start()

    loads[1].wait()

    @pl.loop(0, length_x)
    def _(i):
        for c in range(3):
            YS[0, 0, c, pl.ds(i, 1)] = D[0, c, i, pl.ds(length_y - 1, 1)]
            YS[0, 1, c, pl.ds(i, 1)] = D[0, c, i, pl.ds(0, 1)]

    @pl.when(has_up)
    def _():
        y_up(0).start()

    @pl.when(has_dn)
    def _():
        y_down(0).start()

    def lookup(kinds, table):
        result = jnp.full(kinds.shape, table[0], jnp.float32)
        for kind in range(1, 8):
            result = jnp.where(kinds == kind, table[kind], result)
        return result

    inner_lane = lane_id < length_z - 1
    own_edge = inner_lane & jnp.logical_or(has_up, row_id < length_y - 1)

    @pl.loop(0, length_x)
    def _(i):
        kinds = M[i]
        keep = own_edge & (jnp.logical_or(has_hi, i < last))
        E[i + 1, pl.ds(8, length_y)] = jnp.where(keep, lookup(kinds, moduli), 0.0)
        C[i] = STEP_TIME / lookup(kinds, density)

    @pl.when(is_face)
    def _():
        base = yz * length_y
        side_base = cross * length_y
        pool_lane = lax.broadcasted_iota(jnp.int32, (1, 2 * length_y), 1)

        @pl.when(body == 0)
        def _():
            @pl.loop(0, length_y)
            def _(r):
                wanted = partner[base + r]
                column = jnp.where(
                    (wanted >= base) & (wanted < base + length_y),
                    wanted - base,
                    wanted - side_base + length_y,
                )
                G[pl.ds(r, 1)] = jnp.where(pool_lane == column, 1.0, 0.0)
                ACT[pl.ds(r, 1)] = jnp.full((1, length_z), active[base + r].astype(jnp.float32))

        @pl.when(body == 1)
        def _():
            @pl.loop(0, 2 * length_y)
            def _(q):
                row = jnp.where(q < length_y, base + q, side_base + q - length_y)
                GT[pl.ds(q, 1)] = jnp.where(pool_lane == partner[row] - base, 1.0, 0.0)
                FX[pl.ds(q, 1)] = jnp.full((1, length_z), active[row].astype(jnp.float32))

            turned = GT[...].T[:length_y]
            G[...] = turned
            ACT[...] = jnp.dot(turned, FX[...], preferred_element_type=jnp.float32, precision=HIGHEST)

    @pl.when(has_lo)
    def _():
        m_x.wait_recv()

    @pl.when(has_dn)
    def _():
        m_y.wait_recv()

    @pl.when(has_lo & has_dn)
    def _():
        m_c.wait_recv()

    E[0, pl.ds(8, length_y)] = jnp.where(own_edge & has_lo, lookup(MX[...], moduli), 0.0)
    row_lane = lax.broadcasted_iota(jnp.int32, (length_x, length_z), 1) < length_z - 1
    row_pos = lax.broadcasted_iota(jnp.int32, (length_x, length_z), 0)
    side = jnp.where(
        row_lane & has_dn & jnp.logical_or(has_hi, row_pos < last), lookup(MY[...], moduli), 0.0
    )
    SYL[...] = side
    E[0, pl.ds(7, 1)] = jnp.where(
        inner_lane[:1] & has_lo & has_dn, lookup(MC[pl.ds(7, 1)], moduli), 0.0
    )

    @pl.loop(0, length_x)
    def _(i):
        E[i + 1, pl.ds(7, 1)] = SYL[pl.ds(i, 1)]

    def with_left(value):
        return value + pltpu.roll(value, 1, 1)

    quarter = 0.25 * YIELD_SPAN

    @pl.loop(0, length_x + 1)
    def _(i):
        whole = E[i]
        here = whole[8:]
        behind = pltpu.roll(whole, 1, 0)[8:]
        SX[i] = quarter * with_left(here + behind)

        @pl.when(i > 0)
        def _():
            under = E[i - 1]
            both = whole + under
            SY[i - 1] = quarter * with_left(both[8:])
            SZ[i - 1] = quarter * (both + pltpu.roll(both, 1, 0))[8:]
            SYL[pl.ds(i - 1, 1)] = quarter * with_left(both[7:8])

    loads[2].wait()

    sharp = 1.0 / YIELD_SPAN

    def scaled(s, c, x):
        return D[s, c, x] * sharp

    def node_update(s, c, x, here, pull_x, pull_x_below, extra):
        ahead = pltpu.roll(here, length_y - 1, 0)
        ahead = jnp.where(row_id == length_y - 1, YH[s, 1, c, pl.ds(x, 1)] * sharp, ahead)
        pull_y = SY[x] * jnp.tanh(ahead - here)
        first = SYL[pl.ds(x, 1)] * jnp.tanh(here[:1] - YH[s, 0, c, pl.ds(x, 1)] * sharp)
        below = jnp.where(row_id == 0, first, pltpu.roll(pull_y, 1, 0))
        pull_z = SZ[x] * jnp.tanh(pltpu.roll(here, length_z - 1, 1) - here)
        force = (pull_x - pull_x_below) + (pull_y - below) + (pull_z - pltpu.roll(pull_z, 1, 1))
        if extra is not None:
            force = force + extra
        speed = V[c, x] + C[x] * force
        V[c, x] = speed
        moved = D[s, c, x] + STEP_TIME * speed
        D[s + 1, c, x] = moved
        return moved

    def keep_rows(s, c, x, moved):
        @pl.when(s + 1 < STEPS)
        def _():
            YS[s + 1, 0, c, pl.ds(x, 1)] = moved[length_y - 1 :]
            YS[s + 1, 1, c, pl.ds(x, 1)] = moved[:1]

    def first_layer(s, c):
        here = scaled(s, c, 0)
        pull_below = SX[0] * jnp.tanh(here - XH[s, 0, c] * sharp)
        pull_x = SX[1] * jnp.tanh(scaled(s, c, 1) - here)
        keep_rows(s, c, 0, node_update(s, c, 0, here, pull_x, pull_below, None))

    def last_layer(s, c, extra=None):
        here = scaled(s, c, last)
        pull_below = SX[last] * jnp.tanh(here - scaled(s, c, last - 1))
        pull_x = SX[last + 1] * jnp.tanh(XH[s, 1, c] * sharp - here)
        keep_rows(s, c, last, node_update(s, c, last, here, pull_x, pull_below, extra))

    def matched(s, c):
        pool = CP[s, c].reshape(2 * length_y, length_z)
        return jnp.dot(G[...], pool, preferred_element_type=jnp.float32, precision=HIGHEST)

    column = lane_id.astype(jnp.float32)
    depth = LOG2E / SOFT_WIDTH

    def weights(s):
        own_y = D[s, 1, last] * PLANE
        own_z = (D[s, 2, last] + column) * PLANE
        far_y = matched(s, 1) * PLANE
        far_z = (matched(s, 2) + column) * PLANE

        @pl.loop(0, length_z // GROUP)
        def _(block):
            for k in range(GROUP):
                turn = block * GROUP + k
                along_y = own_y - pltpu.roll(far_y, turn, 1)
                along_z = own_z - pltpu.roll(far_z, turn, 1)
                WT[turn] = jnp.exp2(-(along_y * along_y + along_z * along_z))

    def contact(s):
        own_x = D[s, 0, last] * depth
        far_x = matched(s, 0) * depth

        def group(block, total):
            for k in range(GROUP):
                turn = block * GROUP + k
                squeeze = own_x + pltpu.roll(far_x, turn, 1)
                hard = jnp.maximum(squeeze, 0.0)
                soft = jnp.log(1.0 + jnp.exp2(squeeze - (hard + hard)))
                total = total + WT[turn] * (hard * math.log(2.0) + soft)
            return total

        total = lax.fori_loop(
            0, length_z // GROUP, group, jnp.zeros((length_y, length_z), jnp.float32)
        )
        return total * (ACT[...] * (-PENALTY * SOFT_WIDTH))

    def step(s, carry):
        more = s + 1 < STEPS

        @pl.when(is_face)
        def _():
            for c in (1, 2):
                c_same(s, c, D.at[s, c, last]).wait_recv()
                c_cross(s, c, D.at[s, c, last]).wait_recv()
            weights(s)

        @pl.when(has_dn)
        def _():
            y_up(s).wait_recv()

        @pl.when(has_up)
        def _():
            y_down(s).wait_recv()

        @pl.when(has_hi)
        def _():
            x_down(s, D.at[s, :, 0]).wait_recv()
            for c in range(3):
                last_layer(s, c)

            @pl.when(more)
            def _():
                x_up(s + 1, D.at[s + 1, :, last]).start()

        @pl.when(is_face)
        def _():
            for c in (1, 2):
                last_layer(s, c)

                @pl.when(more)
                def _():
                    c_same(s + 1, c, D.at[s + 1, c, last]).start()
                    c_cross(s + 1, c, D.at[s + 1, c, last]).start()

        @pl.when(has_lo)
        def _():
            x_up(s, D.at[s, :, last]).wait_recv()

        for c in range(3):
            first_layer(s, c)

        @pl.when(more & has_lo)
        def _():
            x_down(s + 1, D.at[s + 1, :, 0]).start()

        for c in range(3):
            here = scaled(s, c, 1)
            pull = SX[1] * jnp.tanh(here - scaled(s, c, 0))

            def layer(x, state):
                here, below = state
                ahead = scaled(s, c, x + 1)
                pull_x = SX[x + 1] * jnp.tanh(ahead - here)
                keep_rows(s, c, x, node_update(s, c, x, here, pull_x, below, None))
                return ahead, pull_x

            lax.fori_loop(1, last, layer, (here, pull))

        @pl.when(is_face)
        def _():
            c_same(s, 0, D.at[s, 0, last]).wait_recv()
            c_cross(s, 0, D.at[s, 0, last]).wait_recv()
            last_layer(s, 0, contact(s))

            @pl.when(more)
            def _():
                c_same(s + 1, 0, D.at[s + 1, 0, last]).start()
                c_cross(s + 1, 0, D.at[s + 1, 0, last]).start()

        @pl.when(more & has_up)
        def _():
            y_up(s + 1).start()

        @pl.when(more & has_dn)
        def _():
            y_down(s + 1).start()

        return carry

    lax.fori_loop(0, STEPS, step, 0)

    stores = [
        pltpu.make_async_copy(D.at[STEPS], out_d.at[0], out_sem.at[0]),
        pltpu.make_async_copy(V, out_v.at[0], out_sem.at[1]),
    ]
    for item in stores:
        item.start()

    @pl.when(has_hi)
    def _():
        m_x.wait_send()

    @pl.when(has_up)
    def _():
        m_y.wait_send()

    @pl.when(has_hi & has_up)
    def _():
        m_c.wait_send()

    def drain(s, carry):
        @pl.when(has_hi)
        def _():
            x_up(s, D.at[s, :, last]).wait_send()

        @pl.when(has_lo)
        def _():
            x_down(s, D.at[s, :, 0]).wait_send()

        @pl.when(has_up)
        def _():
            y_up(s).wait_send()

        @pl.when(has_dn)
        def _():
            y_down(s).wait_send()

        @pl.when(is_face)
        def _():
            for c in range(3):
                c_same(s, c, D.at[s, c, last]).wait_send()
                c_cross(s, c, D.at[s, c, last]).wait_send()

        return carry

    lax.fori_loop(0, STEPS, drain, 0)
    for item in stores:
        item.wait()


def local(displacement, velocity, material, moduli, density, partner, active):
    length_x, length_y, length_z = displacement.shape[2:]
    count_x = lax.axis_size("gx")
    count_y = lax.axis_size("yz")
    f32 = jnp.float32
    i32 = jnp.int32
    layer = (length_y, length_z)
    solid = (length_x,) + layer
    anywhere = pl.BlockSpec(memory_space=pl.ANY)
    scalars = pl.BlockSpec(memory_space=pltpu.SMEM)
    dma = pltpu.SemaphoreType.DMA
    return pl.pallas_call(
        functools.partial(kernel, count_x, count_y, (length_x, length_y, length_z)),
        out_shape=(
            jax.ShapeDtypeStruct(displacement.shape, f32),
            jax.ShapeDtypeStruct(velocity.shape, f32),
        ),
        in_specs=[anywhere] * 3 + [scalars] * 4,
        out_specs=(anywhere, anywhere),
        scratch_shapes=[
            pltpu.VMEM((STEPS + 1, 3) + solid, f32),
            pltpu.VMEM((3,) + solid, f32),
            pltpu.VMEM(solid, i32),
            pltpu.VMEM((length_x + 1, length_y + 8, length_z), f32),
            pltpu.VMEM((length_x + 1,) + layer, f32),
            pltpu.VMEM(solid, f32),
            pltpu.VMEM((length_x, length_z), f32),
            pltpu.VMEM(solid, f32),
            pltpu.VMEM(solid, f32),
            pltpu.VMEM((STEPS, 2, 3) + layer, f32),
            pltpu.VMEM((STEPS, 2, 3, length_x, length_z), f32),
            pltpu.VMEM((STEPS, 2, 3, length_x, length_z), f32),
            pltpu.VMEM(layer, i32),
            pltpu.VMEM((length_x, length_z), i32),
            pltpu.VMEM((8, length_z), i32),
            pltpu.VMEM((length_x, length_z), i32),
            pltpu.VMEM((STEPS, 3, 2) + layer, f32),
            pltpu.VMEM((length_y, 2 * length_y), f32),
            pltpu.VMEM((2 * length_y, 2 * length_y), f32),
            pltpu.VMEM(layer, f32),
            pltpu.VMEM((length_z,) + layer, f32),
            pltpu.VMEM((2 * length_y, length_z), f32),
            dma((3,)), dma((2,)), dma((3,)), dma((3,)),
            dma((STEPS, 2)), dma((STEPS, 2)), dma((STEPS, 2)), dma((STEPS, 2)),
            dma((STEPS, 3, 2)), dma((STEPS, 3, 2)),
        ],
        compiler_params=pltpu.CompilerParams(
            collective_id=0, has_side_effects=True, vmem_limit_bytes=48 * 1024 * 1024
        ),
        name="impact",
    )(displacement, velocity, material, moduli, density, partner, active)


def solution(mesh):
    in_specs = (
        P("body", None, "gx", "yz", None),
        P("body", None, "gx", "yz", None),
        P("body", "gx", "yz", None),
        P(),
        P(),
        P(),
        P(),
    )
    out_specs = (P("body", None, "gx", "yz", None), P("body", None, "gx", "yz", None))
    return jax.shard_map(local, mesh=mesh, in_specs=in_specs, out_specs=out_specs, check_vma=False)
```

time: 188 us -> 78.4 us (0.42); the launches traced: 184 us -> 78.2 us
  other arithmetic: 88.7 us -> 0 us
  Pallas kernels: 0 us -> 70.1 us
  starting transfers between devices: 56.5 us -> 0 us
  waiting for transfers between devices: 22.2 us -> 0 us
  local copies, waits for them, and re-layouts: 12.9 us -> 7.4 us
    pallas_call x0 -> x1, Pallas kernels: none -> 70.1 us  [local(): pl.pallas_call(functools.partial(kernel, count_x, count_y, (length_x, len...]
    ppermute x34 -> x0, starting transfers between devices: 56.5 us -> none  [the longest x8 21.3 us: padded(): lax.ppermute(lax.slice_in_dim(block, 0, width, axis=dim), axis, backward)]
    ppermute x34 -> x0, waiting for transfers between devices: 22.2 us -> none  [the longest x8 12.7 us: shifted_2(): return lax.ppermute(value, axis, pairs)]
    reduce_sum x32 -> x0, other arithmetic: 21.8 us -> none  [per_block(): jnp.sum(pressure, axis=1)]
    dynamic_update_slice x32 -> x0, other arithmetic: 21.3 us -> none  [paired_terms(): pushed, reacted = lax.map(per_block, (own_split, far_split, live_split))]
    mul x15 -> x0, other arithmetic: 15.8 us -> none  [the longest x5 6.36 us: axis_forces(): pulls = stiffness * tension(ahead - displace)]
    add x45 -> x0, other arithmetic: 8.75 us -> none  [the longest x4 5.63 us: local(): displacement = displacement + STEP_TIME * velocity]
    select_n x10 -> x0, other arithmetic: 7.49 us -> none  [the longest x1 6.85 us: local(): elements = jnp.where(inside[None], lookup(material, moduli), 0.0)]
  transfers between devices with their start and end apart: 34 -> 0, of which waited for: 14 -> 0; matrix products, arithmetic and copies ran while one was open for 43% -> 0% of each run, Pallas kernels for 0% -> 0%
where the time goes in v1:
time: 78.4 us; the launch traced here: 78.2 us
  Pallas kernels  70.1 us (89%)
  local copies, waits for them, and re-layouts  7.4 us (9%)
    pallas_call x1, Pallas kernels, local(): pl.pallas_call(functools.partial(kernel, count_x, count_y, (length_x, len...  70.1 us
    unnamed x14, local copies, waits for them, and re-layouts  7.4 us

profile of v1, /device:TPU:249, one launch (start us, length us, event | category | flops | bytes accessed | tf_op | source)
XLA Modules:
  0.0 78.2 jit_solution(12627734442092883298)
XLA Ops:
  0.6 0.0 copy-start
  0.6 1.4 %copy-done = f32[1,3,16,64,128]{4,3,2,1,0:T(8,128)S(1)} copy-done((f32[1,3,16,64,128]{4,3,2,1,0:T(8,128)S(1)}, f32[1,3,16,64,128]{4,3,2,1,0:T(8,128)}, u32[]{:S(2)}) %copy-start) | copy-done | bytes 1572888
  2.0 0.0 copy-start.1
  2.0 1.0 %copy-done.1 = s32[1,16,64,128]{3,2,1,0:T(8,128)S(1)} copy-done((s32[1,16,64,128]{3,2,1,0:T(8,128)S(1)}, s32[1,16,64,128]{3,2,1,0:T(8,128)}, u32[]{:S(2)}) %copy-start.1) | copy-done | bytes 524312
  3.1 0.0 copy-start.2
  3.1 0.7 copy-done.2
  3.8 0.0 copy-start.3
  3.8 0.7 copy-done.3
  4.4 0.0 copy-start.4
  4.4 0.7 copy-done.4
  5.1 0.0 copy-start.5
  5.1 0.7 copy-done.5
  5.8 70.1 %impact.1 = (f32[1,3,16,64,128]{4,3,2,1,0:T(8,128)S(1)}, f32[1,3,16,64,128]{4,3,2,1,0:T(8,128)S(1)}) custom-call(f32[1,3,16,64,128]{4,3,2,1,0:T(8,128)S(1)} %copy-done, f32[1,3,16,64,128]{4,3,2,1,0:T(8,128)} %velo.1, s32[1,16,64,128]{3,2,1,0:T(8,128)S(1)} %copy-done.1, f32[8]{0:T(128)S(1)} %copy-done.4, f32[8]{0:T(128)S(1)} %copy-done.5, s32[256]{0:T(256)S(1)} %copy-done.2, ...), custom_call_target="tpu_custom_call" | custom-call | tf_op jit(solution)/shard_map/impact/pallas_call | solution.py:499
  75.9 1.1 %copy.11 = f32[1,3,16,64,128]{4,3,2,1,0:T(8,128)} copy(f32[1,3,16,64,128]{4,3,2,1,0:T(8,128)S(1)} %get-tuple-element.4) | data formatting | bytes 3145728
  77.0 1.1 %copy.12 = f32[1,3,16,64,128]{4,3,2,1,0:T(8,128)} copy(f32[1,3,16,64,128]{4,3,2,1,0:T(8,128)S(1)} %get-tuple-element.5) | data formatting | bytes 3145728
Async XLA Ops:
  0.6 1.4 %copy-start = (f32[1,3,16,64,128]{4,3,2,1,0:T(8,128)S(1)}, f32[1,3,16,64,128]{4,3,2,1,0:T(8,128)}, u32[]{:S(2)}) copy-start(f32[1,3,16,64,128]{4,3,2,1,0:T(8,128)} %disp.1) | copy-start | bytes 4718596
  2.0 1.0 %copy-start.1 = (s32[1,16,64,128]{3,2,1,0:T(8,128)S(1)}, s32[1,16,64,128]{3,2,1,0:T(8,128)}, u32[]{:S(2)}) copy-start(s32[1,16,64,128]{3,2,1,0:T(8,128)} %mat_hbm.1) | copy-start | bytes 1572868
  3.1 0.7 copy-start.2
  3.8 0.7 copy-start.3
  4.4 0.7 copy-start.4
  5.1 0.7 copy-start.5

commit v2 on v1

--- a/solution.py
+++ b/solution.py
@@ -24,10 +24,11 @@
 
 def kernel(
     count_x, count_y, dims,
-    disp, velo, mat_hbm, moduli, density, partner, active,
+    disp, velo, mat_hbm, moduli_hbm, density_hbm, partner_hbm, active_hbm,
     out_d, out_v,
-    D, V, M, E, SX, SY, SYL, SZ, C,
-    XH, YH, YS, MX, MY, MC, MYS, CP, G, GT, ACT, WT, FX,
+    D, V, M, E, SX, SY, SYL, SZ, SZB, C, PX,
+    XH, YH, YS, MX, MY, MC, MYS, OT, CP, W, WTURN, ACT, WT, FY, FZ, FX,
+    moduli, density, partner, active,
     load_sem, out_sem, m_send, m_recv, x_send, x_recv, y_send, y_recv, c_send, c_recv,
 ):
     length_x, length_y, length_z = dims
@@ -59,6 +60,10 @@
         pltpu.make_async_copy(mat_hbm.at[0], M, load_sem.at[0]),
         pltpu.make_async_copy(disp.at[0], D.at[0], load_sem.at[1]),
         pltpu.make_async_copy(velo.at[0], V, load_sem.at[2]),
+        pltpu.make_async_copy(moduli_hbm, moduli, load_sem.at[3]),
+        pltpu.make_async_copy(density_hbm, density, load_sem.at[4]),
+        pltpu.make_async_copy(partner_hbm, partner, load_sem.at[5]),
+        pltpu.make_async_copy(active_hbm, active, load_sem.at[6]),
     ]
     for item in loads:
         item.start()
@@ -97,11 +102,11 @@
     def y_down(s):
         return remote(YS.at[s, 1], YH.at[s, 1], y_send.at[s, 1], y_recv.at[s, 1], down)
 
-    def c_same(s, c, source):
-        return remote(source, CP.at[s, c, 0], c_send.at[s, c, 0], c_recv.at[s, c, 0], same_peer)
-
-    def c_cross(s, c, source):
-        return remote(source, CP.at[s, c, 1], c_send.at[s, c, 1], c_recv.at[s, c, 1], cross_peer)
+    def c_same(s, c):
+        return remote(OT.at[s, c], CP.at[s, c, 0], c_send.at[s, c, 0], c_recv.at[s, c, 0], same_peer)
+
+    def c_cross(s, c):
+        return remote(OT.at[s, c], CP.at[s, c, 1], c_send.at[s, c, 1], c_recv.at[s, c, 1], cross_peer)
 
     m_x = remote(mat_hbm.at[0, last], MX, m_send.at[0], m_recv.at[0], high)
     m_y = remote(MYS, MY, m_send.at[1], m_recv.at[1], up)
@@ -116,11 +121,17 @@
     def _():
         x_down(0, disp.at[0, :, 0]).start()
 
-    @pl.when(is_face)
-    def _():
-        for c in (1, 2, 0):
-            c_same(0, c, disp.at[0, c, last]).start()
-            c_cross(0, c, disp.at[0, c, last]).start()
+    half = length_z // 2
+    low_lanes = lane_id < half
+
+    def turn_face(s, c):
+        own = D[s, c, last]
+        turned = jnp.concatenate([own, own], axis=0).T
+        OT[s, c] = jnp.where(low_lanes, turned[:half], turned[half:])
+
+    def send_face(s, c):
+        c_same(s, c).start()
+        c_cross(s, c).start()
 
     @pl.when(jnp.logical_not(has_lo))
     def _():
@@ -166,8 +177,17 @@
     @pl.loop(0, length_x)
     def _(i):
         for c in range(3):
-            YS[0, 0, c, pl.ds(i, 1)] = D[0, c, i, pl.ds(length_y - 1, 1)]
-            YS[0, 1, c, pl.ds(i, 1)] = D[0, c, i, pl.ds(0, 1)]
+            doubled = D[0, c, i] * (1.0 / YIELD_SPAN)
+            D[0, c, i] = doubled
+            YS[0, 0, c, pl.ds(i, 1)] = doubled[length_y - 1 :]
+            YS[0, 1, c, pl.ds(i, 1)] = doubled[:1]
+
+    @pl.when(is_face)
+    def _():
+        for c in (1, 2, 0):
+            turn_face(0, c)
+        for c in (1, 2, 0):
+            send_face(0, c)
 
     @pl.when(has_up)
     def _():
@@ -176,6 +196,9 @@
     @pl.when(has_dn)
     def _():
         y_down(0).start()
+
+    for item in loads[3:]:
+        item.wait()
 
     def lookup(kinds, table):
         result = jnp.full(kinds.shape, table[0], jnp.float32)
@@ -191,38 +214,48 @@
         kinds = M[i]
         keep = own_edge & (jnp.logical_or(has_hi, i < last))
         E[i + 1, pl.ds(8, length_y)] = jnp.where(keep, lookup(kinds, moduli), 0.0)
-        C[i] = STEP_TIME / lookup(kinds, density)
+        C[i] = (STEP_TIME * STEP_TIME / YIELD_SPAN) / lookup(kinds, density)
 
     @pl.when(is_face)
     def _():
         base = yz * length_y
         side_base = cross * length_y
-        pool_lane = lax.broadcasted_iota(jnp.int32, (1, 2 * length_y), 1)
+        lanes = 2 * length_y
+        out_lane = lax.broadcasted_iota(jnp.int32, (1, lanes), 1)
 
         @pl.when(body == 0)
         def _():
-            @pl.loop(0, length_y)
-            def _(r):
-                wanted = partner[base + r]
-                column = jnp.where(
-                    (wanted >= base) & (wanted < base + length_y),
-                    wanted - base,
-                    wanted - side_base + length_y,
+            pool_lane = lax.broadcasted_iota(jnp.int32, (1, 2 * lanes), 1)
+
+            def fill(row, total):
+                upper = jnp.where(row >= length_y, 1, 0)
+                own = base + row - upper * length_y
+                wanted = partner[own]
+                near = (wanted >= base) & (wanted < base + length_y)
+                column = jnp.where(near, wanted - base, wanted - side_base + lanes) + upper * length_y
+                WTURN[pl.ds(row, 1)] = jnp.where(pool_lane == column, 1.0, 0.0)
+                return total + jnp.where(out_lane == row, active[own].astype(jnp.float32), 0.0)
+
+            live = lax.fori_loop(0, lanes, fill, jnp.zeros((1, lanes), jnp.float32))
+            ACT[...] = live * (-PENALTY * SOFT_WIDTH)
+            W[...] = WTURN[...].T
+
+        @pl.when(body == 1)
+        def _():
+            def fill(row, total):
+                upper = jnp.where(lax.rem(row, lanes) >= length_y, 1, 0)
+                spot = lax.rem(row, length_y)
+                own = jnp.where(row < lanes, base, side_base) + spot
+                wanted = partner[own] - base
+                match = (out_lane == wanted + upper * length_y) & (
+                    (out_lane >= upper * length_y) & (out_lane < (upper + 1) * length_y)
                 )
-                G[pl.ds(r, 1)] = jnp.where(pool_lane == column, 1.0, 0.0)
-                ACT[pl.ds(r, 1)] = jnp.full((1, length_z), active[base + r].astype(jnp.float32))
-
-        @pl.when(body == 1)
-        def _():
-            @pl.loop(0, 2 * length_y)
-            def _(q):
-                row = jnp.where(q < length_y, base + q, side_base + q - length_y)
-                GT[pl.ds(q, 1)] = jnp.where(pool_lane == partner[row] - base, 1.0, 0.0)
-                FX[pl.ds(q, 1)] = jnp.full((1, length_z), active[row].astype(jnp.float32))
-
-            turned = GT[...].T[:length_y]
-            G[...] = turned
-            ACT[...] = jnp.dot(turned, FX[...], preferred_element_type=jnp.float32, precision=HIGHEST)
+                line = jnp.where(match, 1.0, 0.0)
+                W[pl.ds(row, 1)] = line
+                return total + line * active[own].astype(jnp.float32)
+
+            live = lax.fori_loop(0, 2 * lanes, fill, jnp.zeros((1, lanes), jnp.float32))
+            ACT[...] = live * (-PENALTY * SOFT_WIDTH)
 
     @pl.when(has_lo)
     def _():
@@ -268,88 +301,111 @@
             under = E[i - 1]
             both = whole + under
             SY[i - 1] = quarter * with_left(both[8:])
-            SZ[i - 1] = quarter * (both + pltpu.roll(both, 1, 0))[8:]
+            edge = quarter * (both + pltpu.roll(both, 1, 0))[8:]
+            SZ[i - 1] = edge
+            SZB[i - 1] = pltpu.roll(edge, 1, 1)
             SYL[pl.ds(i - 1, 1)] = quarter * with_left(both[7:8])
 
     loads[2].wait()
 
-    sharp = 1.0 / YIELD_SPAN
-
-    def scaled(s, c, x):
-        return D[s, c, x] * sharp
-
-    def node_update(s, c, x, here, pull_x, pull_x_below, extra):
+    @pl.loop(0, length_x)
+    def _(i):
+        for c in range(3):
+            V[c, i] = V[c, i] * (STEP_TIME / YIELD_SPAN)
+
+    def node_update(s, c, x, here, pull_x, pull_x_below, extra=None):
         ahead = pltpu.roll(here, length_y - 1, 0)
-        ahead = jnp.where(row_id == length_y - 1, YH[s, 1, c, pl.ds(x, 1)] * sharp, ahead)
+        ahead = jnp.where(row_id == length_y - 1, YH[s, 1, c, pl.ds(x, 1)], ahead)
         pull_y = SY[x] * jnp.tanh(ahead - here)
-        first = SYL[pl.ds(x, 1)] * jnp.tanh(here[:1] - YH[s, 0, c, pl.ds(x, 1)] * sharp)
+        first = SYL[pl.ds(x, 1)] * jnp.tanh(here[:1] - YH[s, 0, c, pl.ds(x, 1)])
         below = jnp.where(row_id == 0, first, pltpu.roll(pull_y, 1, 0))
         pull_z = SZ[x] * jnp.tanh(pltpu.roll(here, length_z - 1, 1) - here)
-        force = (pull_x - pull_x_below) + (pull_y - below) + (pull_z - pltpu.roll(pull_z, 1, 1))
+        pull_z_below = SZB[x] * jnp.tanh(here - pltpu.roll(here, 1, 1))
+        force = (pull_x - pull_x_below) + (pull_y - below) + (pull_z - pull_z_below)
         if extra is not None:
             force = force + extra
         speed = V[c, x] + C[x] * force
         V[c, x] = speed
-        moved = D[s, c, x] + STEP_TIME * speed
+        moved = here + speed
         D[s + 1, c, x] = moved
-        return moved
-
-    def keep_rows(s, c, x, moved):
-        @pl.when(s + 1 < STEPS)
-        def _():
-            YS[s + 1, 0, c, pl.ds(x, 1)] = moved[length_y - 1 :]
-            YS[s + 1, 1, c, pl.ds(x, 1)] = moved[:1]
+        YS[s + 1, 0, c, pl.ds(x, 1)] = moved[length_y - 1 :]
+        YS[s + 1, 1, c, pl.ds(x, 1)] = moved[:1]
+
+    def raw_scale(s):
+        return jnp.where(s == 0, 1.0 / YIELD_SPAN, 1.0)
 
     def first_layer(s, c):
-        here = scaled(s, c, 0)
-        pull_below = SX[0] * jnp.tanh(here - XH[s, 0, c] * sharp)
-        pull_x = SX[1] * jnp.tanh(scaled(s, c, 1) - here)
-        keep_rows(s, c, 0, node_update(s, c, 0, here, pull_x, pull_below, None))
+        here = D[s, c, 0]
+        pull_below = SX[0] * jnp.tanh(here - XH[s, 0, c] * raw_scale(s))
+        pull_x = SX[1] * jnp.tanh(D[s, c, 1] - here)
+        PX[c] = pull_x
+        node_update(s, c, 0, here, pull_x, pull_below)
 
     def last_layer(s, c, extra=None):
-        here = scaled(s, c, last)
-        pull_below = SX[last] * jnp.tanh(here - scaled(s, c, last - 1))
-        pull_x = SX[last + 1] * jnp.tanh(XH[s, 1, c] * sharp - here)
-        keep_rows(s, c, last, node_update(s, c, last, here, pull_x, pull_below, extra))
+        here = D[s, c, last]
+        pull_below = SX[last] * jnp.tanh(here - D[s, c, last - 1])
+        pull_x = SX[last + 1] * jnp.tanh(XH[s, 1, c] * raw_scale(s) - here)
+        node_update(s, c, last, here, pull_x, pull_below, extra)
 
     def matched(s, c):
-        pool = CP[s, c].reshape(2 * length_y, length_z)
-        return jnp.dot(G[...], pool, preferred_element_type=jnp.float32, precision=HIGHEST)
-
-    column = lane_id.astype(jnp.float32)
-    depth = LOG2E / SOFT_WIDTH
+        pool = jnp.concatenate([CP[s, c, 0], CP[s, c, 1]], axis=1)
+        high = pool.astype(jnp.bfloat16)
+        rest = pool - high.astype(jnp.float32)
+        middle = rest.astype(jnp.bfloat16)
+        tail = (rest - middle.astype(jnp.float32)).astype(jnp.bfloat16)
+        pick = W[...].astype(jnp.bfloat16)
+        parts = [
+            jnp.dot(part, pick, preferred_element_type=jnp.float32) for part in (high, middle, tail)
+        ]
+        return (parts[0] + parts[1]) + parts[2]
+
+    def spread(ref, lower, upper):
+        ref[pl.ds(0, half)] = lower
+        ref[pl.ds(half, half)] = upper
+        ref[pl.ds(2 * half, half)] = lower
+
+    half_rows = row_id[:half]
+    half_lanes = lane_id[:half]
+    place = (half_rows + jnp.where(half_lanes < half, 0, half)).astype(jnp.float32)
+    place_other = (half_rows + jnp.where(half_lanes < half, half, 0)).astype(jnp.float32)
+    depth = LOG2E / SOFT_WIDTH * YIELD_SPAN
 
     def weights(s):
-        own_y = D[s, 1, last] * PLANE
-        own_z = (D[s, 2, last] + column) * PLANE
-        far_y = matched(s, 1) * PLANE
-        far_z = (matched(s, 2) + column) * PLANE
+        far_y = matched(s, 1) * (PLANE * YIELD_SPAN)
+        far_z = matched(s, 2) * YIELD_SPAN
+        spread(FY, far_y, pltpu.roll(far_y, half, 1))
+        spread(FZ, (far_z + place) * PLANE, (pltpu.roll(far_z, half, 1) + place_other) * PLANE)
+        own_y = OT[s, 1] * (PLANE * YIELD_SPAN)
+        own_z = (OT[s, 2] * YIELD_SPAN + place) * PLANE
 
         @pl.loop(0, length_z // GROUP)
         def _(block):
             for k in range(GROUP):
                 turn = block * GROUP + k
-                along_y = own_y - pltpu.roll(far_y, turn, 1)
-                along_z = own_z - pltpu.roll(far_z, turn, 1)
-                WT[turn] = jnp.exp2(-(along_y * along_y + along_z * along_z))
+                along_y = own_y - FY[pl.ds(turn, half)]
+                along_z = own_z - FZ[pl.ds(turn, half)]
+                WT[turn] = jnp.exp2((0.0 - along_y * along_y) - along_z * along_z)
 
     def contact(s):
-        own_x = D[s, 0, last] * depth
         far_x = matched(s, 0) * depth
+        spread(FX, far_x, pltpu.roll(far_x, half, 1))
+        own_x = OT[s, 0] * depth
 
         def group(block, total):
             for k in range(GROUP):
                 turn = block * GROUP + k
-                squeeze = own_x + pltpu.roll(far_x, turn, 1)
+                squeeze = own_x + FX[pl.ds(turn, half)]
                 hard = jnp.maximum(squeeze, 0.0)
                 soft = jnp.log(1.0 + jnp.exp2(squeeze - (hard + hard)))
                 total = total + WT[turn] * (hard * math.log(2.0) + soft)
             return total
 
         total = lax.fori_loop(
-            0, length_z // GROUP, group, jnp.zeros((length_y, length_z), jnp.float32)
+            0, length_z // GROUP, group, jnp.zeros((half, length_z), jnp.float32)
         )
-        return total * (ACT[...] * (-PENALTY * SOFT_WIDTH))
+        total = total * ACT[...]
+        turned = jnp.concatenate([total, total], axis=0).T
+        return jnp.where(low_lanes, turned[:length_y], turned[length_y:])
 
     def step(s, carry):
         more = s + 1 < STEPS
@@ -357,8 +413,8 @@
         @pl.when(is_face)
         def _():
             for c in (1, 2):
-                c_same(s, c, D.at[s, c, last]).wait_recv()
-                c_cross(s, c, D.at[s, c, last]).wait_recv()
+                c_same(s, c).wait_recv()
+                c_cross(s, c).wait_recv()
             weights(s)
 
         @pl.when(has_dn)
@@ -383,11 +439,12 @@
         def _():
             for c in (1, 2):
                 last_layer(s, c)
-
-                @pl.when(more)
-                def _():
-                    c_same(s + 1, c, D.at[s + 1, c, last]).start()
-                    c_cross(s + 1, c, D.at[s + 1, c, last]).start()
+                turn_face(s + 1, c)
+
+            @pl.when(more)
+            def _():
+                for c in (1, 2):
+                    send_face(s + 1, c)
 
         @pl.when(has_lo)
         def _():
@@ -400,29 +457,27 @@
         def _():
             x_down(s + 1, D.at[s + 1, :, 0]).start()
 
-        for c in range(3):
-            here = scaled(s, c, 1)
-            pull = SX[1] * jnp.tanh(here - scaled(s, c, 0))
-
-            def layer(x, state):
-                here, below = state
-                ahead = scaled(s, c, x + 1)
-                pull_x = SX[x + 1] * jnp.tanh(ahead - here)
-                keep_rows(s, c, x, node_update(s, c, x, here, pull_x, below, None))
-                return ahead, pull_x
-
-            lax.fori_loop(1, last, layer, (here, pull))
+        @pl.loop(0, (last - 1) // 2)
+        def _(pair):
+            for offset in range(2):
+                x = 2 * pair + 1 + offset
+                for c in range(3):
+                    here = D[s, c, x]
+                    pull_x = SX[x + 1] * jnp.tanh(D[s, c, x + 1] - here)
+                    below = PX[c]
+                    PX[c] = pull_x
+                    node_update(s, c, x, here, pull_x, below)
 
         @pl.when(is_face)
         def _():
-            c_same(s, 0, D.at[s, 0, last]).wait_recv()
-            c_cross(s, 0, D.at[s, 0, last]).wait_recv()
+            c_same(s, 0).wait_recv()
+            c_cross(s, 0).wait_recv()
             last_layer(s, 0, contact(s))
 
             @pl.when(more)
             def _():
-                c_same(s + 1, 0, D.at[s + 1, 0, last]).start()
-                c_cross(s + 1, 0, D.at[s + 1, 0, last]).start()
+                turn_face(s + 1, 0)
+                send_face(s + 1, 0)
 
         @pl.when(more & has_up)
         def _():
@@ -475,8 +530,8 @@
         @pl.when(is_face)
         def _():
             for c in range(3):
-                c_same(s, c, D.at[s, c, last]).wait_send()
-                c_cross(s, c, D.at[s, c, last]).wait_send()
+                c_same(s, c).wait_send()
+                c_cross(s, c).wait_send()
 
         return carry
 
@@ -494,15 +549,16 @@
     layer = (length_y, length_z)
     solid = (length_x,) + layer
     anywhere = pl.BlockSpec(memory_space=pl.ANY)
-    scalars = pl.BlockSpec(memory_space=pltpu.SMEM)
+    far_memory = pl.BlockSpec(memory_space=pltpu.HBM)
     dma = pltpu.SemaphoreType.DMA
-    return pl.pallas_call(
+    half = length_z // 2
+    scaled_d, scaled_v = pl.pallas_call(
         functools.partial(kernel, count_x, count_y, (length_x, length_y, length_z)),
         out_shape=(
             jax.ShapeDtypeStruct(displacement.shape, f32),
             jax.ShapeDtypeStruct(velocity.shape, f32),
         ),
-        in_specs=[anywhere] * 3 + [scalars] * 4,
+        in_specs=[far_memory] * 7,
         out_specs=(anywhere, anywhere),
         scratch_shapes=[
             pltpu.VMEM((STEPS + 1, 3) + solid, f32),
@@ -514,20 +570,29 @@
             pltpu.VMEM((length_x, length_z), f32),
             pltpu.VMEM(solid, f32),
             pltpu.VMEM(solid, f32),
+            pltpu.VMEM(solid, f32),
+            pltpu.VMEM((3,) + layer, f32),
             pltpu.VMEM((STEPS, 2, 3) + layer, f32),
             pltpu.VMEM((STEPS, 2, 3, length_x, length_z), f32),
-            pltpu.VMEM((STEPS, 2, 3, length_x, length_z), f32),
+            pltpu.VMEM((STEPS + 1, 2, 3, length_x, length_z), f32),
             pltpu.VMEM(layer, i32),
             pltpu.VMEM((length_x, length_z), i32),
             pltpu.VMEM((8, length_z), i32),
             pltpu.VMEM((length_x, length_z), i32),
-            pltpu.VMEM((STEPS, 3, 2) + layer, f32),
-            pltpu.VMEM((length_y, 2 * length_y), f32),
-            pltpu.VMEM((2 * length_y, 2 * length_y), f32),
-            pltpu.VMEM(layer, f32),
-            pltpu.VMEM((length_z,) + layer, f32),
-            pltpu.VMEM((2 * length_y, length_z), f32),
-            dma((3,)), dma((2,)), dma((3,)), dma((3,)),
+            pltpu.VMEM((STEPS + 1, 3, half, 2 * length_y), f32),
+            pltpu.VMEM((STEPS, 3, 2, half, 2 * length_y), f32),
+            pltpu.VMEM((4 * length_y, 2 * length_y), f32),
+            pltpu.VMEM((2 * length_y, 4 * length_y), f32),
+            pltpu.VMEM((1, 2 * length_y), f32),
+            pltpu.VMEM((length_z, half, 2 * length_y), f32),
+            pltpu.VMEM((3 * half, 2 * length_y), f32),
+            pltpu.VMEM((3 * half, 2 * length_y), f32),
+            pltpu.VMEM((3 * half, 2 * length_y), f32),
+            pltpu.SMEM(moduli.shape, f32),
+            pltpu.SMEM(density.shape, f32),
+            pltpu.SMEM(partner.shape, i32),
+            pltpu.SMEM(active.shape, i32),
+            dma((7,)), dma((2,)), dma((3,)), dma((3,)),
             dma((STEPS, 2)), dma((STEPS, 2)), dma((STEPS, 2)), dma((STEPS, 2)),
             dma((STEPS, 3, 2)), dma((STEPS, 3, 2)),
         ],
@@ -535,7 +600,11 @@
             collective_id=0, has_side_effects=True, vmem_limit_bytes=48 * 1024 * 1024
         ),
         name="impact",
-    )(displacement, velocity, material, moduli, density, partner, active)
+    )(*[
+        pltpu.with_memory_space_constraint(item, pltpu.HBM)
+        for item in (displacement, velocity, material, moduli, density, partner, active)
+    ])
+    return scaled_d * YIELD_SPAN, scaled_v * (YIELD_SPAN / STEP_TIME)
 
 
 def solution(mesh):

time: 78.4 us -> 43.8 us (0.56)
  Pallas kernels: 70.1 us -> 40.8 us
  local copies, waits for them, and re-layouts: 7.4 us -> 0 us
  other arithmetic: 0 us -> 2.23 us
    pallas_call x1, Pallas kernels: 70.1 us -> 40.8 us  [local(): pl.pallas_call(functools.partial(kernel, count_x, count_y, (length_x, len...]
    unnamed x14 -> x0, local copies, waits for them, and re-layouts: 7.4 us -> none
    mul x0 -> x1, other arithmetic: none -> 2.23 us  [local(): return (scaled_d * YIELD_SPAN, scaled_v * (YIELD_SPAN / STEP_TIME))]
where the time goes in v2:
time: 43.8 us; the launch traced here: 43.7 us
  Pallas kernels  40.8 us (93%)
  other arithmetic  2.23 us (5%)
  between operations  0.64 us (1%)
    pallas_call x1, Pallas kernels, local(): pl.pallas_call(functools.partial(kernel, count_x, count_y, (length_x, len...  40.8 us
    mul x1, other arithmetic, local(): return (scaled_d * YIELD_SPAN, scaled_v * (YIELD_SPAN / STEP_TIME))  2.23 us

profile of v2, /device:TPU:249, one launch (start us, length us, event | category | flops | bytes accessed | tf_op | source)
XLA Modules:
  0.0 43.7 jit_solution(13909258099690237951)
XLA Ops:
  0.6 40.8 %impact.1 = (f32[1,3,16,64,128]{4,3,2,1,0:T(8,128)S(1)}, f32[1,3,16,64,128]{4,3,2,1,0:T(8,128)S(1)}) custom-call(f32[1,3,16,64,128]{4,3,2,1,0:T(8,128)} %disp.1, f32[1,3,16,64,128]{4,3,2,1,0:T(8,128)} %velo.1, s32[1,16,64,128]{3,2,1,0:T(8,128)} %mat_hbm.1, f32[8]{0:T(128)} %moduli_hbm.1, f32[8]{0:T(128)} %density_hbm.1, s32[256]{0:T(256)} %partner_hbm.1, ...), custom_call_target="tpu_custom_call" | custom-call | tf_op jit(solution)/shard_map/impact/pallas_call | solution.py:555
  41.5 2.2 %broadcast_multiply_fusion = (f32[1,3,16,64,128]{4,3,2,1,0:T(8,128)}, f32[1,3,16,64,128]{4,3,2,1,0:T(8,128)}) fusion(f32[1,3,16,64,128]{4,3,2,1,0:T(8,128)S(1)} %get-tuple-element.5, f32[1,3,16,64,128]{4,3,2,1,0:T(8,128)S(1)} %get-tuple-element.4), kind=kLoop, calls=%fused_computation | loop fusion | flops 786432 | bytes 6291456 | tf_op jit(solution)/shard_map/mul | solution.py:607

commit v3 on v2

--- a/solution.py
+++ b/solution.py
@@ -16,7 +16,7 @@
 KERNEL_WIDTH = 1.5
 LOG2E = 1.0 / math.log(2.0)
 PLANE = math.sqrt(LOG2E / (2.0 * KERNEL_WIDTH * KERNEL_WIDTH))
-GROUP = 8
+GROUP = 16
 
 MESH = pl.DeviceIdType.MESH
 HIGHEST = lax.Precision.HIGHEST
@@ -27,9 +27,9 @@
     disp, velo, mat_hbm, moduli_hbm, density_hbm, partner_hbm, active_hbm,
     out_d, out_v,
     D, V, M, E, SX, SY, SYL, SZ, SZB, C, PX,
-    XH, YH, YS, MX, MY, MC, MYS, OT, CP, W, WTURN, ACT, WT, FY, FZ, FX,
-    moduli, density, partner, active,
-    load_sem, out_sem, m_send, m_recv, x_send, x_recv, y_send, y_recv, c_send, c_recv,
+    XH, YH, YS, YLH, YLS, MX, MY, MC, MYS, CS, CP, GIVE, TAKE, ACT, WT, FY, FZ, FX,
+    partner, active, moduli, density,
+    load_sem, out_sem, m_send, m_recv, x_send, x_recv, y_send, y_recv, l_send, l_recv, c_send, c_recv,
 ):
     length_x, length_y, length_z = dims
     last = length_x - 1
@@ -44,6 +44,7 @@
     cross = lax.rem(yz + 1 - 2 * body + count_y, count_y)
     other = 1 - body
 
+    quota = length_y // 2
     low = {"gx": gx - 1}
     high = {"gx": gx + 1}
     down = {"yz": yz - 1}
@@ -90,11 +91,17 @@
             device_id=device, device_id_type=MESH,
         )
 
-    def x_up(s, source):
-        return remote(source, XH.at[s, 0], x_send.at[s, 0], x_recv.at[s, 0], high)
-
-    def x_down(s, source):
-        return remote(source, XH.at[s, 1], x_send.at[s, 1], x_recv.at[s, 1], low)
+    def x_up(s, c, source):
+        return remote(source, XH.at[s, 0, c], x_send.at[s, 0, c], x_recv.at[s, 0, c], high)
+
+    def x_down(s, c, source):
+        return remote(source, XH.at[s, 1, c], x_send.at[s, 1, c], x_recv.at[s, 1, c], low)
+
+    def late_up(s):
+        return remote(YLS.at[s, 0], YLH.at[s, 0], l_send.at[s, 0], l_recv.at[s, 0], up)
+
+    def late_down(s):
+        return remote(YLS.at[s, 1], YLH.at[s, 1], l_send.at[s, 1], l_recv.at[s, 1], down)
 
     def y_up(s):
         return remote(YS.at[s, 0], YH.at[s, 0], y_send.at[s, 0], y_recv.at[s, 0], up)
@@ -103,10 +110,16 @@
         return remote(YS.at[s, 1], YH.at[s, 1], y_send.at[s, 1], y_recv.at[s, 1], down)
 
     def c_same(s, c):
-        return remote(OT.at[s, c], CP.at[s, c, 0], c_send.at[s, c, 0], c_recv.at[s, c, 0], same_peer)
+        return remote(
+            CS.at[s, c, pl.ds(0, quota)], CP.at[s, c, pl.ds(0, quota)],
+            c_send.at[s, c, 0], c_recv.at[s, c, 0], same_peer,
+        )
 
     def c_cross(s, c):
-        return remote(OT.at[s, c], CP.at[s, c, 1], c_send.at[s, c, 1], c_recv.at[s, c, 1], cross_peer)
+        return remote(
+            CS.at[s, c, pl.ds(quota, quota)], CP.at[s, c, pl.ds(quota, quota)],
+            c_send.at[s, c, 1], c_recv.at[s, c, 1], cross_peer,
+        )
 
     m_x = remote(mat_hbm.at[0, last], MX, m_send.at[0], m_recv.at[0], high)
     m_y = remote(MYS, MY, m_send.at[1], m_recv.at[1], up)
@@ -115,19 +128,38 @@
     @pl.when(has_hi)
     def _():
         m_x.start()
-        x_up(0, disp.at[0, :, last]).start()
+        for c in range(3):
+            x_up(0, c, disp.at[0, c, last]).start()
 
     @pl.when(has_lo)
     def _():
-        x_down(0, disp.at[0, :, 0]).start()
+        for c in range(3):
+            x_down(0, c, disp.at[0, c, 0]).start()
 
     half = length_z // 2
     low_lanes = lane_id < half
 
-    def turn_face(s, c):
-        own = D[s, c, last]
-        turned = jnp.concatenate([own, own], axis=0).T
-        OT[s, c] = jnp.where(low_lanes, turned[:half], turned[half:])
+    def exact_pick(choice, value):
+        high_part = value.astype(jnp.bfloat16)
+        rest = value - high_part.astype(jnp.float32)
+        middle = rest.astype(jnp.bfloat16)
+        tail = (rest - middle.astype(jnp.float32)).astype(jnp.bfloat16)
+        upper_parts = jnp.concatenate([high_part, middle], axis=0)
+        lower_parts = jnp.concatenate([tail, jnp.zeros_like(tail)], axis=0)
+        return jnp.dot(choice, upper_parts, preferred_element_type=jnp.float32) + jnp.dot(
+            choice, lower_parts, preferred_element_type=jnp.float32
+        )
+
+    def turned_pair(value):
+        turned = jnp.concatenate([value, value], axis=0).T
+        return turned[:half], turned[half:]
+
+    def own_face(s, c):
+        lower, upper = turned_pair(D[s, c, last])
+        return jnp.where(low_lanes, lower, upper)
+
+    def pack_face(s, c):
+        CS[s, c] = exact_pick(GIVE[...], D[s, c, last])
 
     def send_face(s, c):
         c_same(s, c).start()
@@ -144,11 +176,13 @@
     @pl.when(jnp.logical_not(has_dn))
     def _():
         YH[:, 0] = jnp.zeros((STEPS, 3, length_x, length_z), jnp.float32)
+        YLH[:, 0] = jnp.zeros((STEPS, 8, length_z), jnp.float32)
         MY[...] = jnp.zeros((length_x, length_z), jnp.int32)
 
     @pl.when(jnp.logical_not(has_up))
     def _():
         YH[:, 1] = jnp.zeros((STEPS, 3, length_x, length_z), jnp.float32)
+        YLH[:, 1] = jnp.zeros((STEPS, 8, length_z), jnp.float32)
 
     @pl.when(jnp.logical_not(has_lo))
     def _():
@@ -171,6 +205,63 @@
     @pl.when(has_hi & has_up)
     def _():
         m_c.start()
+
+    for item in loads[3:]:
+        item.wait()
+
+    @pl.when(is_face)
+    def _():
+        base = yz * length_y
+        size = (2 * length_y, 2 * length_y)
+        rows = lax.broadcasted_iota(jnp.int32, size, 0)
+        lanes = lax.broadcasted_iota(jnp.int32, size, 1)
+
+        def publish(mate_col, mate_row, live):
+            near_col = (mate_col >= base) & (mate_col < base + length_y)
+            near_row = (mate_row >= base) & (mate_row < base + length_y)
+            shift_col = jnp.where(near_col, 0.0, 1.0)
+            shift_row = jnp.where(near_row, 0.0, 1.0)
+            alike = shift_col == shift_row
+            before = jnp.where(alike & (mate_row < mate_col) & (lanes < length_y), 1.0, 0.0)
+            spot = jnp.sum(before, axis=1, keepdims=True) + quota * shift_col
+            name = lanes.astype(jnp.float32)
+            TAKE[...] = jnp.where(
+                (name == spot) | (name == spot + float(length_y)), 1.0, 0.0
+            )[:length_y].astype(jnp.bfloat16)
+            earlier = jnp.where(alike & (rows < lanes) & (rows < length_y), 1.0, 0.0)
+            slot = jnp.sum(earlier, axis=0, keepdims=True) + quota * shift_row
+            single = jnp.where(rows.astype(jnp.float32) == slot, 1.0, 0.0)
+            GIVE[...] = jnp.where(lanes < length_y, single, pltpu.roll(single, length_y, 1))[
+                :length_y
+            ].astype(jnp.bfloat16)
+            ACT[...] = live[:length_y] * (-PENALTY * SOFT_WIDTH)
+
+        @pl.when(body == 0)
+        def _():
+            def own_block(table):
+                line = jnp.where(yz < 2, table[pl.ds(0, 1)], table[pl.ds(1, 1)])
+                moved = jnp.where(lax.rem(yz, 2) == 0, line, pltpu.roll(line, half, 1))
+                return jnp.broadcast_to(moved.astype(jnp.float32), size)
+
+            across = own_block(partner)
+            publish(across.T.astype(jnp.int32), across.astype(jnp.int32), own_block(active).T)
+
+        @pl.when(body == 1)
+        def _():
+            mate = jnp.zeros((2 * length_y, 1), jnp.float32)
+            live = jnp.zeros((2 * length_y, 1), jnp.float32)
+            for part in range(2):
+                hit = jnp.where(partner[pl.ds(part, 1)] == rows + base, 1.0, 0.0)
+                name = (lanes + part * length_z).astype(jnp.float32)
+                mate = mate + jnp.sum(hit * name, axis=1, keepdims=True)
+                live = live + jnp.sum(
+                    hit * active[pl.ds(part, 1)].astype(jnp.float32), axis=1, keepdims=True
+                )
+            down_rows = jnp.broadcast_to(mate, size)
+            publish(
+                down_rows.astype(jnp.int32), down_rows.T.astype(jnp.int32),
+                jnp.broadcast_to(live, size),
+            )
 
     loads[1].wait()
 
@@ -182,10 +273,22 @@
             YS[0, 0, c, pl.ds(i, 1)] = doubled[length_y - 1 :]
             YS[0, 1, c, pl.ds(i, 1)] = doubled[:1]
 
+    def send_late(s):
+        @pl.when(has_up)
+        def _():
+            late_up(s).start()
+
+        @pl.when(has_dn)
+        def _():
+            late_down(s).start()
+
     @pl.when(is_face)
     def _():
+        YLS[0, 0, pl.ds(0, 1)] = D[0, 0, last, pl.ds(length_y - 1, 1)]
+        YLS[0, 1, pl.ds(0, 1)] = D[0, 0, last, pl.ds(0, 1)]
+        send_late(0)
         for c in (1, 2, 0):
-            turn_face(0, c)
+            pack_face(0, c)
         for c in (1, 2, 0):
             send_face(0, c)
 
@@ -196,9 +299,6 @@
     @pl.when(has_dn)
     def _():
         y_down(0).start()
-
-    for item in loads[3:]:
-        item.wait()
 
     def lookup(kinds, table):
         result = jnp.full(kinds.shape, table[0], jnp.float32)
@@ -215,47 +315,6 @@
         keep = own_edge & (jnp.logical_or(has_hi, i < last))
         E[i + 1, pl.ds(8, length_y)] = jnp.where(keep, lookup(kinds, moduli), 0.0)
         C[i] = (STEP_TIME * STEP_TIME / YIELD_SPAN) / lookup(kinds, density)
-
-    @pl.when(is_face)
-    def _():
-        base = yz * length_y
-        side_base = cross * length_y
-        lanes = 2 * length_y
-        out_lane = lax.broadcasted_iota(jnp.int32, (1, lanes), 1)
-
-        @pl.when(body == 0)
-        def _():
-            pool_lane = lax.broadcasted_iota(jnp.int32, (1, 2 * lanes), 1)
-
-            def fill(row, total):
-                upper = jnp.where(row >= length_y, 1, 0)
-                own = base + row - upper * length_y
-                wanted = partner[own]
-                near = (wanted >= base) & (wanted < base + length_y)
-                column = jnp.where(near, wanted - base, wanted - side_base + lanes) + upper * length_y
-                WTURN[pl.ds(row, 1)] = jnp.where(pool_lane == column, 1.0, 0.0)
-                return total + jnp.where(out_lane == row, active[own].astype(jnp.float32), 0.0)
-
-            live = lax.fori_loop(0, lanes, fill, jnp.zeros((1, lanes), jnp.float32))
-            ACT[...] = live * (-PENALTY * SOFT_WIDTH)
-            W[...] = WTURN[...].T
-
-        @pl.when(body == 1)
-        def _():
-            def fill(row, total):
-                upper = jnp.where(lax.rem(row, lanes) >= length_y, 1, 0)
-                spot = lax.rem(row, length_y)
-                own = jnp.where(row < lanes, base, side_base) + spot
-                wanted = partner[own] - base
-                match = (out_lane == wanted + upper * length_y) & (
-                    (out_lane >= upper * length_y) & (out_lane < (upper + 1) * length_y)
-                )
-                line = jnp.where(match, 1.0, 0.0)
-                W[pl.ds(row, 1)] = line
-                return total + line * active[own].astype(jnp.float32)
-
-            live = lax.fori_loop(0, 2 * lanes, fill, jnp.zeros((1, lanes), jnp.float32))
-            ACT[...] = live * (-PENALTY * SOFT_WIDTH)
 
     @pl.when(has_lo)
     def _():
@@ -313,23 +372,31 @@
         for c in range(3):
             V[c, i] = V[c, i] * (STEP_TIME / YIELD_SPAN)
 
-    def node_update(s, c, x, here, pull_x, pull_x_below, extra=None):
+    def node_update(s, c, x, here, pull_x, pull_x_below, push=None):
+        if push is None:
+            row_up, row_down = YH[s, 1, c, pl.ds(x, 1)], YH[s, 0, c, pl.ds(x, 1)]
+        else:
+            row_up, row_down = YLH[s, 1, pl.ds(0, 1)], YLH[s, 0, pl.ds(0, 1)]
         ahead = pltpu.roll(here, length_y - 1, 0)
-        ahead = jnp.where(row_id == length_y - 1, YH[s, 1, c, pl.ds(x, 1)], ahead)
+        ahead = jnp.where(row_id == length_y - 1, row_up, ahead)
         pull_y = SY[x] * jnp.tanh(ahead - here)
-        first = SYL[pl.ds(x, 1)] * jnp.tanh(here[:1] - YH[s, 0, c, pl.ds(x, 1)])
+        first = SYL[pl.ds(x, 1)] * jnp.tanh(here[:1] - row_down)
         below = jnp.where(row_id == 0, first, pltpu.roll(pull_y, 1, 0))
         pull_z = SZ[x] * jnp.tanh(pltpu.roll(here, length_z - 1, 1) - here)
         pull_z_below = SZB[x] * jnp.tanh(here - pltpu.roll(here, 1, 1))
         force = (pull_x - pull_x_below) + (pull_y - below) + (pull_z - pull_z_below)
-        if extra is not None:
-            force = force + extra
+        if push is not None:
+            force = force + push
         speed = V[c, x] + C[x] * force
         V[c, x] = speed
         moved = here + speed
         D[s + 1, c, x] = moved
-        YS[s + 1, 0, c, pl.ds(x, 1)] = moved[length_y - 1 :]
-        YS[s + 1, 1, c, pl.ds(x, 1)] = moved[:1]
+        if push is None:
+            YS[s + 1, 0, c, pl.ds(x, 1)] = moved[length_y - 1 :]
+            YS[s + 1, 1, c, pl.ds(x, 1)] = moved[:1]
+        else:
+            YLS[s + 1, 0, pl.ds(0, 1)] = moved[length_y - 1 :]
+            YLS[s + 1, 1, pl.ds(0, 1)] = moved[:1]
 
     def raw_scale(s):
         return jnp.where(s == 0, 1.0 / YIELD_SPAN, 1.0)
@@ -341,42 +408,37 @@
         PX[c] = pull_x
         node_update(s, c, 0, here, pull_x, pull_below)
 
-    def last_layer(s, c, extra=None):
+    def last_layer(s, c, push=None):
         here = D[s, c, last]
         pull_below = SX[last] * jnp.tanh(here - D[s, c, last - 1])
         pull_x = SX[last + 1] * jnp.tanh(XH[s, 1, c] * raw_scale(s) - here)
-        node_update(s, c, last, here, pull_x, pull_below, extra)
+        node_update(s, c, last, here, pull_x, pull_below, push)
 
     def matched(s, c):
-        pool = jnp.concatenate([CP[s, c, 0], CP[s, c, 1]], axis=1)
-        high = pool.astype(jnp.bfloat16)
-        rest = pool - high.astype(jnp.float32)
-        middle = rest.astype(jnp.bfloat16)
-        tail = (rest - middle.astype(jnp.float32)).astype(jnp.bfloat16)
-        pick = W[...].astype(jnp.bfloat16)
-        parts = [
-            jnp.dot(part, pick, preferred_element_type=jnp.float32) for part in (high, middle, tail)
-        ]
-        return (parts[0] + parts[1]) + parts[2]
+        return turned_pair(exact_pick(TAKE[...], CP[s, c]))
 
     def spread(ref, lower, upper):
-        ref[pl.ds(0, half)] = lower
-        ref[pl.ds(half, half)] = upper
-        ref[pl.ds(2 * half, half)] = lower
-
-    half_rows = row_id[:half]
-    half_lanes = lane_id[:half]
-    place = (half_rows + jnp.where(half_lanes < half, 0, half)).astype(jnp.float32)
-    place_other = (half_rows + jnp.where(half_lanes < half, half, 0)).astype(jnp.float32)
+        near = jnp.where(low_lanes, lower, upper)
+        other_half = jnp.where(low_lanes, upper, lower)
+        ref[pl.ds(0, half)] = near
+        ref[pl.ds(half, half)] = other_half
+        ref[pl.ds(2 * half, half)] = near
+
+    row_place = row_id.astype(jnp.float32)
+    place = row_place + jnp.where(low_lanes, 0.0, float(half))
     depth = LOG2E / SOFT_WIDTH * YIELD_SPAN
 
     def weights(s):
-        far_y = matched(s, 1) * (PLANE * YIELD_SPAN)
-        far_z = matched(s, 2) * YIELD_SPAN
-        spread(FY, far_y, pltpu.roll(far_y, half, 1))
-        spread(FZ, (far_z + place) * PLANE, (pltpu.roll(far_z, half, 1) + place_other) * PLANE)
-        own_y = OT[s, 1] * (PLANE * YIELD_SPAN)
-        own_z = (OT[s, 2] * YIELD_SPAN + place) * PLANE
+        lower, upper = matched(s, 1)
+        spread(FY, lower * (PLANE * YIELD_SPAN), upper * (PLANE * YIELD_SPAN))
+        lower, upper = matched(s, 2)
+        spread(
+            FZ,
+            (lower * YIELD_SPAN + row_place) * PLANE,
+            (upper * YIELD_SPAN + (row_place + float(half))) * PLANE,
+        )
+        own_y = own_face(s, 1) * (PLANE * YIELD_SPAN)
+        own_z = (own_face(s, 2) * YIELD_SPAN + place) * PLANE
 
         @pl.loop(0, length_z // GROUP)
         def _(block):
@@ -386,37 +448,27 @@
                 along_z = own_z - FZ[pl.ds(turn, half)]
                 WT[turn] = jnp.exp2((0.0 - along_y * along_y) - along_z * along_z)
 
-    def contact(s):
-        far_x = matched(s, 0) * depth
-        spread(FX, far_x, pltpu.roll(far_x, half, 1))
-        own_x = OT[s, 0] * depth
+    def contact(s, own_x):
+        lower, upper = matched(s, 0)
+        spread(FX, lower * depth, upper * depth)
 
         def group(block, total):
             for k in range(GROUP):
                 turn = block * GROUP + k
                 squeeze = own_x + FX[pl.ds(turn, half)]
-                hard = jnp.maximum(squeeze, 0.0)
-                soft = jnp.log(1.0 + jnp.exp2(squeeze - (hard + hard)))
-                total = total + WT[turn] * (hard * math.log(2.0) + soft)
+                soft = jnp.log(1.0 + jnp.exp2(jnp.minimum(squeeze, 64.0)))
+                total = total + WT[turn] * jnp.maximum(soft, squeeze * math.log(2.0))
             return total
 
         total = lax.fori_loop(
             0, length_z // GROUP, group, jnp.zeros((half, length_z), jnp.float32)
         )
-        total = total * ACT[...]
-        turned = jnp.concatenate([total, total], axis=0).T
-        return jnp.where(low_lanes, turned[:length_y], turned[length_y:])
+        lower, upper = turned_pair(total)
+        return jnp.where(low_lanes, lower, upper) * ACT[...]
 
     def step(s, carry):
         more = s + 1 < STEPS
 
-        @pl.when(is_face)
-        def _():
-            for c in (1, 2):
-                c_same(s, c).wait_recv()
-                c_cross(s, c).wait_recv()
-            weights(s)
-
         @pl.when(has_dn)
         def _():
             y_up(s).wait_recv()
@@ -427,19 +479,22 @@
 
         @pl.when(has_hi)
         def _():
-            x_down(s, D.at[s, :, 0]).wait_recv()
+            for c in range(3):
+                x_down(s, c, D.at[s, c, 0]).wait_recv()
             for c in range(3):
                 last_layer(s, c)
 
             @pl.when(more)
             def _():
-                x_up(s + 1, D.at[s + 1, :, last]).start()
+                for c in range(3):
+                    x_up(s + 1, c, D.at[s + 1, c, last]).start()
 
         @pl.when(is_face)
         def _():
             for c in (1, 2):
                 last_layer(s, c)
-                turn_face(s + 1, c)
+            for c in (1, 2):
+                pack_face(s + 1, c)
 
             @pl.when(more)
             def _():
@@ -448,14 +503,16 @@
 
         @pl.when(has_lo)
         def _():
-            x_up(s, D.at[s, :, last]).wait_recv()
+            for c in range(3):
+                x_up(s, c, D.at[s, c, last]).wait_recv()
 
         for c in range(3):
             first_layer(s, c)
 
         @pl.when(more & has_lo)
         def _():
-            x_down(s + 1, D.at[s + 1, :, 0]).start()
+            for c in range(3):
+                x_down(s + 1, c, D.at[s + 1, c, 0]).start()
 
         @pl.loop(0, (last - 1) // 2)
         def _(pair):
@@ -468,24 +525,41 @@
                     PX[c] = pull_x
                     node_update(s, c, x, here, pull_x, below)
 
+        @pl.when(more & has_up)
+        def _():
+            y_up(s + 1).start()
+
+        @pl.when(more & has_dn)
+        def _():
+            y_down(s + 1).start()
+
         @pl.when(is_face)
         def _():
+            for c in (1, 2):
+                c_same(s, c).wait_recv()
+                c_cross(s, c).wait_recv()
+            weights(s)
+
+            @pl.when(has_dn)
+            def _():
+                late_up(s).wait_recv()
+
+            @pl.when(has_up)
+            def _():
+                late_down(s).wait_recv()
+
+            own_x = own_face(s, 0) * depth
             c_same(s, 0).wait_recv()
             c_cross(s, 0).wait_recv()
-            last_layer(s, 0, contact(s))
+            last_layer(s, 0, contact(s, own_x))
+
+            pack_face(s + 1, 0)
 
             @pl.when(more)
             def _():
-                turn_face(s + 1, 0)
                 send_face(s + 1, 0)
-
-        @pl.when(more & has_up)
-        def _():
-            y_up(s + 1).start()
-
-        @pl.when(more & has_dn)
-        def _():
-            y_down(s + 1).start()
+                send_late(s + 1)
+
 
         return carry
 
@@ -513,11 +587,13 @@
     def drain(s, carry):
         @pl.when(has_hi)
         def _():
-            x_up(s, D.at[s, :, last]).wait_send()
+            for c in range(3):
+                x_up(s, c, D.at[s, c, last]).wait_send()
 
         @pl.when(has_lo)
         def _():
-            x_down(s, D.at[s, :, 0]).wait_send()
+            for c in range(3):
+                x_down(s, c, D.at[s, c, 0]).wait_send()
 
         @pl.when(has_up)
         def _():
@@ -532,6 +608,14 @@
             for c in range(3):
                 c_same(s, c).wait_send()
                 c_cross(s, c).wait_send()
+
+            @pl.when(has_up)
+            def _():
+                late_up(s).wait_send()
+
+            @pl.when(has_dn)
+            def _():
+                late_down(s).wait_send()
 
         return carry
 
@@ -575,24 +659,27 @@
             pltpu.VMEM((STEPS, 2, 3) + layer, f32),
             pltpu.VMEM((STEPS, 2, 3, length_x, length_z), f32),
             pltpu.VMEM((STEPS + 1, 2, 3, length_x, length_z), f32),
+            pltpu.VMEM((STEPS, 2, 8, length_z), f32),
+            pltpu.VMEM((STEPS + 1, 2, 8, length_z), f32),
             pltpu.VMEM(layer, i32),
             pltpu.VMEM((length_x, length_z), i32),
             pltpu.VMEM((8, length_z), i32),
             pltpu.VMEM((length_x, length_z), i32),
-            pltpu.VMEM((STEPS + 1, 3, half, 2 * length_y), f32),
-            pltpu.VMEM((STEPS, 3, 2, half, 2 * length_y), f32),
-            pltpu.VMEM((4 * length_y, 2 * length_y), f32),
-            pltpu.VMEM((2 * length_y, 4 * length_y), f32),
-            pltpu.VMEM((1, 2 * length_y), f32),
+            pltpu.VMEM((STEPS + 1, 3) + layer, f32),
+            pltpu.VMEM((STEPS, 3) + layer, f32),
+            pltpu.VMEM((length_y, 2 * length_y), jnp.bfloat16),
+            pltpu.VMEM((length_y, 2 * length_y), jnp.bfloat16),
+            pltpu.VMEM(layer, f32),
             pltpu.VMEM((length_z, half, 2 * length_y), f32),
             pltpu.VMEM((3 * half, 2 * length_y), f32),
             pltpu.VMEM((3 * half, 2 * length_y), f32),
             pltpu.VMEM((3 * half, 2 * length_y), f32),
+            pltpu.VMEM((2, length_z), i32),
+            pltpu.VMEM((2, length_z), i32),
             pltpu.SMEM(moduli.shape, f32),
             pltpu.SMEM(density.shape, f32),
-            pltpu.SMEM(partner.shape, i32),
-            pltpu.SMEM(active.shape, i32),
             dma((7,)), dma((2,)), dma((3,)), dma((3,)),
+            dma((STEPS, 2, 3)), dma((STEPS, 2, 3)),
             dma((STEPS, 2)), dma((STEPS, 2)), dma((STEPS, 2)), dma((STEPS, 2)),
             dma((STEPS, 3, 2)), dma((STEPS, 3, 2)),
         ],
@@ -602,7 +689,10 @@
         name="impact",
     )(*[
         pltpu.with_memory_space_constraint(item, pltpu.HBM)
-        for item in (displacement, velocity, material, moduli, density, partner, active)
+        for item in (
+            displacement, velocity, material, moduli, density,
+            partner.reshape(2, length_z), active.reshape(2, length_z),
+        )
     ])
     return scaled_d * YIELD_SPAN, scaled_v * (YIELD_SPAN / STEP_TIME)
 

time: 43.8 us -> 38.9 us (0.89)
  Pallas kernels: 40.8 us -> 36 us
    pallas_call x1, Pallas kernels: 40.8 us -> 36 us  [local(): pl.pallas_call(functools.partial(kernel, count_x, count_y, (length_x, len...]
where the time goes in v3:
time: 38.9 us; the launch traced here: 38.8 us
  Pallas kernels  36 us (93%)
  other arithmetic  2.23 us (6%)
  between operations  0.64 us (2%)
    pallas_call x1, Pallas kernels, local(): pl.pallas_call(functools.partial(kernel, count_x, count_y, (length_x, len...  36 us
    mul x1, other arithmetic, local(): return (scaled_d * YIELD_SPAN, scaled_v * (YIELD_SPAN / STEP_TIME))  2.23 us

profile of v3, /device:TPU:249, one launch (start us, length us, event | category | flops | bytes accessed | tf_op | source)
XLA Modules:
  0.0 38.8 jit_solution(5789337409861703161)
XLA Ops:
  0.6 36.0 %impact.1 = (f32[1,3,16,64,128]{4,3,2,1,0:T(8,128)S(1)}, f32[1,3,16,64,128]{4,3,2,1,0:T(8,128)S(1)}) custom-call(f32[1,3,16,64,128]{4,3,2,1,0:T(8,128)} %disp.1, f32[1,3,16,64,128]{4,3,2,1,0:T(8,128)} %velo.1, s32[1,16,64,128]{3,2,1,0:T(8,128)} %mat_hbm.1, f32[8]{0:T(128)} %moduli_hbm.1, f32[8]{0:T(128)} %density_hbm.1, s32[2,128]{1,0:T(2,128)} %bitcast.2, ...), custom_call_target="tpu_custom_call" | custom-call | tf_op jit(solution)/shard_map/impact/pallas_call | solution.py:639
  36.6 2.2 %broadcast_multiply_fusion = (f32[1,3,16,64,128]{4,3,2,1,0:T(8,128)}, f32[1,3,16,64,128]{4,3,2,1,0:T(8,128)}) fusion(f32[1,3,16,64,128]{4,3,2,1,0:T(8,128)S(1)} %get-tuple-element.5, f32[1,3,16,64,128]{4,3,2,1,0:T(8,128)S(1)} %get-tuple-element.4), kind=kLoop, calls=%fused_computation | loop fusion | flops 786432 | bytes 6291456 | tf_op jit(solution)/shard_map/mul | solution.py:697

commit v4 on v3

--- a/solution.py
+++ b/solution.py
@@ -17,6 +17,7 @@
 LOG2E = 1.0 / math.log(2.0)
 PLANE = math.sqrt(LOG2E / (2.0 * KERNEL_WIDTH * KERNEL_WIDTH))
 GROUP = 16
+LAYERS = 7
 
 MESH = pl.DeviceIdType.MESH
 HIGHEST = lax.Precision.HIGHEST
@@ -496,11 +497,6 @@
             for c in (1, 2):
                 pack_face(s + 1, c)
 
-            @pl.when(more)
-            def _():
-                for c in (1, 2):
-                    send_face(s + 1, c)
-
         @pl.when(has_lo)
         def _():
             for c in range(3):
@@ -514,10 +510,10 @@
             for c in range(3):
                 x_down(s + 1, c, D.at[s + 1, c, 0]).start()
 
-        @pl.loop(0, (last - 1) // 2)
-        def _(pair):
-            for offset in range(2):
-                x = 2 * pair + 1 + offset
+        @pl.loop(0, (last - 1) // LAYERS)
+        def _(pack):
+            for offset in range(LAYERS):
+                x = LAYERS * pack + 1 + offset
                 for c in range(3):
                     here = D[s, c, x]
                     pull_x = SX[x + 1] * jnp.tanh(D[s, c, x + 1] - here)
@@ -547,6 +543,11 @@
             @pl.when(has_up)
             def _():
                 late_down(s).wait_recv()
+
+            @pl.when(more)
+            def _():
+                for c in (1, 2):
+                    send_face(s + 1, c)
 
             own_x = own_face(s, 0) * depth
             c_same(s, 0).wait_recv()

time: 38.9 us -> 38.1 us (0.979)
  Pallas kernels: 36 us -> 35.2 us
    pallas_call x1, Pallas kernels: 36 us -> 35.2 us  [local(): pl.pallas_call(functools.partial(kernel, count_x, count_y, (length_x, len...]
where the time goes in v4:
time: 38.1 us
  Pallas kernels  35.2 us (92%)
  other arithmetic  2.23 us (6%)
  between operations  0.64 us (2%)
    pallas_call x1, Pallas kernels, local(): pl.pallas_call(functools.partial(kernel, count_x, count_y, (length_x, len...  35.2 us
    mul x1, other arithmetic, local(): return (scaled_d * YIELD_SPAN, scaled_v * (YIELD_SPAN / STEP_TIME))  2.23 us

profile of v4, /device:TPU:249, one launch (start us, length us, event | category | flops | bytes accessed | tf_op | source)
XLA Modules:
  0.0 38.1 jit_solution(8393024409724670696)
XLA Ops:
  0.6 35.2 %impact.1 = (f32[1,3,16,64,128]{4,3,2,1,0:T(8,128)S(1)}, f32[1,3,16,64,128]{4,3,2,1,0:T(8,128)S(1)}) custom-call(f32[1,3,16,64,128]{4,3,2,1,0:T(8,128)} %disp.1, f32[1,3,16,64,128]{4,3,2,1,0:T(8,128)} %velo.1, s32[1,16,64,128]{3,2,1,0:T(8,128)} %mat_hbm.1, f32[8]{0:T(128)} %moduli_hbm.1, f32[8]{0:T(128)} %density_hbm.1, s32[2,128]{1,0:T(2,128)} %bitcast.2, ...), custom_call_target="tpu_custom_call" | custom-call | tf_op jit(solution)/shard_map/impact/pallas_call | solution.py:640
  35.8 2.2 %broadcast_multiply_fusion = (f32[1,3,16,64,128]{4,3,2,1,0:T(8,128)}, f32[1,3,16,64,128]{4,3,2,1,0:T(8,128)}) fusion(f32[1,3,16,64,128]{4,3,2,1,0:T(8,128)S(1)} %get-tuple-element.5, f32[1,3,16,64,128]{4,3,2,1,0:T(8,128)S(1)} %get-tuple-element.4), kind=kLoop, calls=%fused_computation | loop fusion | flops 786432 | bytes 6291456 | tf_op jit(solution)/shard_map/mul | solution.py:698
